TPU v7x, 512 devices: a whole 4x4x16 slice. The times are simulated.
512 devices in a mesh: cls: 32 (over z, x_hi), ptcl: 16 (over y, x_lo, core).
Axes of the slice: x: 4 (x_hi: 2, x_lo: 2; x = x_hi * 2 + x_lo), y: 4, z: 16, core: 2. Of those that a mesh axis runs over, the one named last changes fastest.
Arguments:
- images: bfloat16 [2048, 2048], P('cls', 'ptcl'), may hold values from -64 to 64
- references: bfloat16 [128, 2048], P('cls'), may hold values from -1 to 1
- log_prior: bfloat16 [128], P('cls'), may hold values from -1.5 to 0
- defocus: float32 [32], replicated, may hold values from 1.5 to 6
- groups: int32 [2048], P('cls'), may hold values from 0 to 31, as said below
Outputs:
- new_references: float32 [128, 2048], P('cls', 'ptcl')
- class_share: float32 [128], P('cls')
Inputs may be any that keep to these rules, and one draw needn't show every extreme that they name: `groups`: every CTF group holds at least one particle.
All inputs are finite; a program needn't handle non-finite values.
Results may differ from a plain program's by a relative error of at most 0.0065.
Values may be sent and summed in bfloat16 or wider, within the bound.
A program may use at most 64 MiB of HBM per device.

v0:
```python
import math

import jax
import jax.numpy as jnp
from jax import lax
from jax.sharding import PartitionSpec as P

SIDE = 32
ROT = 36
GROUPS = 32


def pixel_coords(pixels):
    center = SIDE // 2
    across = (pixels % SIDE - center).astype(jnp.float32)
    down = (pixels // SIDE - center).astype(jnp.float32)
    return (across, down)


def rotation_weights(out_pixels, rot_ids):
    angles = 2.0 * math.pi * rot_ids.astype(jnp.float32) / ROT
    cosine = jnp.cos(angles)[:, None, None]
    sine_val = jnp.sin(angles)[:, None, None]
    out_across, out_down = pixel_coords(out_pixels)
    in_across, in_down = pixel_coords(jnp.arange(SIDE * SIDE, dtype=jnp.int32))
    source_across = cosine * out_across[None, :, None] + sine_val * out_down[None, :, None]
    source_down = -sine_val * out_across[None, :, None] + cosine * out_down[None, :, None]
    first = jnp.maximum(0.0, 1.0 - jnp.abs(source_across - in_across[None, None, :]))
    second = jnp.maximum(0.0, 1.0 - jnp.abs(source_down - in_down[None, None, :]))
    return first * second


def contrast_values(defocus, pixels):
    across, down = pixel_coords(pixels)
    radius_sq = (across * across + down * down) / float((SIDE // 2) ** 2)
    phase_shift = math.pi * defocus[:, None] * radius_sq[None, :]
    return -(0.99499 * jnp.sin(phase_shift) + 0.1 * jnp.cos(phase_shift))


def normalized(logits):
    peak = jnp.max(logits, axis=1, keepdims=True)
    expo = jnp.exp(logits - peak)
    return (expo / jnp.sum(expo, axis=1, keepdims=True)).astype(jnp.bfloat16)


def project_back(table_half, gathered):
    high_part = gathered.astype(jnp.bfloat16)
    low_part = (gathered - high_part.astype(jnp.float32)).astype(jnp.bfloat16)
    first = jnp.einsum("rqp,krqc->kpc", table_half, high_part, preferred_element_type=jnp.float32)
    second = jnp.einsum("rqp,krqc->kpc", table_half, low_part, preferred_element_type=jnp.float32)
    return first + second


def scores_of(weighted_rows, turned, contrast, selector):
    highest = lax.Precision.HIGHEST
    rows = turned.shape[0] * turned.shape[1]
    width = turned.shape[2]
    flat = turned.reshape(rows, 2 * width)
    matched = lax.dot_general(
        weighted_rows, flat, (((1,), (1,)), ((), ())), preferred_element_type=jnp.float32
    )
    turned_wide = turned.astype(jnp.float32)
    power = jnp.sum(turned_wide * turned_wide, axis=3).reshape(rows, width)
    group_penalty = lax.dot_general(
        contrast * contrast, power, (((1,), (1,)), ((), ())), precision=highest
    )
    penalty = jnp.dot(selector, group_penalty, precision=highest)
    return matched - 0.5 * penalty


def on_device(images, references, log_prior, defocus, groups):
    highest = lax.Precision.HIGHEST
    pix_count = SIDE * SIDE
    particles = images.shape[0]
    local_pixels = images.shape[1] // 2
    class_count = references.shape[0] * lax.axis_size("cls")
    selector = (groups[:, None] == jnp.arange(GROUPS, dtype=jnp.int32)[None, :]).astype(jnp.float32)
    all_refs, all_prior = (
        lax.all_gather(references, "cls", axis=0, tiled=True),
        lax.all_gather(log_prior, "cls", axis=0, tiled=True),
    )
    prior_cols = jnp.repeat(all_prior.astype(jnp.float32), ROT)
    first_pixel = lax.axis_index("ptcl") * local_pixels
    out_pixels = first_pixel + jnp.arange(local_pixels, dtype=jnp.int32)
    table_half = rotation_weights(out_pixels, jnp.arange(ROT, dtype=jnp.int32)).astype(jnp.bfloat16)
    contrast = contrast_values(defocus, out_pixels)
    particle_contrast = jnp.dot(selector, contrast, precision=highest)
    weighted = (
        images.reshape(particles, local_pixels, 2).astype(jnp.float32)
        * particle_contrast[:, :, None]
    ).astype(jnp.bfloat16)
    contrast_sq = (particle_contrast * particle_contrast).astype(jnp.bfloat16)
    stacked = jnp.concatenate([weighted, contrast_sq[:, :, None]], axis=2).reshape(
        particles, 3 * local_pixels
    )
    turned = jnp.einsum(
        "rqp,kpt->krqt",
        table_half,
        all_refs.reshape(class_count, pix_count, 2),
        preferred_element_type=jnp.float32,
    ).astype(jnp.bfloat16)
    partial_scores = scores_of(
        weighted.reshape(particles, 2 * local_pixels), turned, contrast, selector
    )
    summed_scores = lax.psum(partial_scores, "ptcl")
    weights = normalized(summed_scores + prior_cols[None, :])
    accumulated = lax.dot_general(
        weights, stacked, (((0,), (0,)), ((), ())), preferred_element_type=jnp.float32
    )
    back = project_back(table_half, accumulated.reshape(class_count, ROT, local_pixels, 3))
    back = back.reshape(class_count, 3 * pix_count)
    occupancy = jnp.sum(
        weights.reshape(particles, class_count, ROT), axis=(0, 2), dtype=jnp.float32
    )
    owned, owned_counts = (
        lax.psum_scatter(back, "cls", scatter_dimension=0, tiled=True),
        lax.psum_scatter(occupancy, "cls", scatter_dimension=0, tiled=True),
    )
    owned = lax.psum_scatter(owned, "ptcl", scatter_dimension=1, tiled=True)
    owned = owned.reshape(owned.shape[0], local_pixels, 3)
    updated = (owned[:, :, :2] / (owned[:, :, 2:] + 1.0)).reshape(owned.shape[0], 2 * local_pixels)
    class_share = owned_counts * (class_count / (particles * lax.axis_size("cls")))
    return (updated, class_share)


def solution(mesh):
    return jax.shard_map(
        on_device,
        mesh=mesh,
        in_specs=(P("cls", "ptcl"), P("cls", None), P("cls"), P(), P("cls")),
        out_specs=(P("cls", "ptcl"), P("cls")),
        check_vma=False,
    )
```

profile of v0, /device:TPU:1, one launch (start us, length us, event | category | flops | bytes accessed | tf_op | source)
XLA Modules:
  0.0 725.3 jit_solution(735948788386528686)
XLA Ops:
  7.4 72.3 %all-gather = bf16[32,4,2048]{2,1,0:T(4,128)(2,1)S(1)} all-gather(bf16[1,4,2048]{2,1,0:T(4,128)(2,1)} %bitcast.69), channel_id=1, replica_groups=mesh['cls'=32,'ptcl'=16] {'cls'}, dimensions={0}, use_global_device_ids=true | all-gather | bytes 540672 | tf_op jit(solution)/shard_map/all_gather | solution.py:79
  79.7 27.0 %copy.28 = bf16[32,4,2048]{1,0,2:T(8,128)(2,1)} copy(bf16[32,4,2048]{2,1,0:T(4,128)(2,1)S(1)} %all-gather) | data formatting | bytes 1048576 | tf_op jit(solution)/shard_map/all_gather | solution.py:79
  106.7 30.7 %reshape.281 = bf16[128,1024,2]{0,2,1:T(2,128)(2,1)S(1)} reshape(bf16[32,4,2048]{1,0,2:T(8,128)(2,1)} %copy.28) | data formatting | bytes 1048576 | tf_op jit(solution)/shard_map/reshape | solution.py:99
  137.4 0.4 copy.29
  137.9 4.8 multiply_reduce_fusion
  142.7 3.6 copy.30
  146.4 9.6 %reshape.282 = bf16[4608,128]{0,1:T(8,128)(2,1)} reshape(bf16[128,36,64,2]{1,0,3,2:T(8,128)(2,1)} %copy.30) | data formatting | bytes 2359296 | tf_op jit(solution)/shard_map/reshape | solution.py:58
  156.4 2.3 copy.31
  158.7 1.5 reshape.283
  160.2 4.3 fusion.33
  165.0 1.7 fusion
  167.0 0.6 fusion.71
  168.5 58.7 %all-reduce = bf16[128]{0:T(256)(128)(2,1)S(1)} all-reduce(bf16[128]{0:T(256)(128)(2,1)S(1)} %dynamic-update-slice), channel_id=1, replica_groups=mesh['cls'=32,'ptcl'=16] {'cls'}, use_global_device_ids=true, to_apply=%add | all-reduce | flops 128 | bytes 512
  227.7 83.1 %all-reduce.6.cloned.1.call-done = f32[64,4608]{1,0:T(8,128)} async-done(((f32[64,4608]{1,0:T(8,128)}), f32[64,4608]{1,0:T(8,128)}) %all-reduce.6.cloned.1.call-update) | async-done | bytes 1179664 | tf_op jit(solution)/shard_map/psum | solution.py:105
  310.9 1.4 add_reduce_fusion
  312.3 1.6 fusion.17
  314.0 1.6 convert_reduce_fusion
  315.6 5.6 reshape.303
  321.2 1.3 copy.41
  322.5 0.6 fusion.22
  323.1 3.7 fusion.2
  326.9 4.9 fusion.8
  331.8 1.9 copy.36
  333.7 1.6 reshape.285
  336.3 64.8 %all-reduce.2 = f32[128]{0:T(128)S(1)} all-reduce(f32[128]{0:T(128)S(1)} %reduce_sum.38), channel_id=4, replica_groups=mesh['cls'=32,'ptcl'=16] {'cls'}, use_global_device_ids=true, to_apply=%region_8.9.clone | all-reduce | flops 128 | bytes 1024
  401.1 227.9 %all-reduce.8.cloned.1.call-done = f32[128,3072]{0,1:T(8,128)} async-done(((f32[128,3072]{0,1:T(8,128)}), f32[128,3072]{0,1:T(8,128)}) %all-reduce.8.cloned.1.call-update) | async-done | bytes 1572880
  629.0 3.0 constant_dynamic-slice_fusion
  632.0 0.6 dynamic-slice_multiply_fusion
  632.6 83.5 %reduce-scatter.3.cloned.1.call-done = f32[4,192]{0,1:T(8,128)} async-done(((f32[4,3072]{0,1:T(8,128)}), f32[4,192]{0,1:T(8,128)}) %reduce-scatter.3.cloned.1.call-update) | async-done | bytes 3088 | tf_op jit(solution)/shard_map/reduce_scatter | solution.py:119
  716.1 1.0 copy.37
  717.6 0.5 copy.38
  718.1 0.7 copy.39
  (45 shorter events, 2.8 us)
Async XLA Ops:
  7.2 303.7 %all-reduce.6.cloned.1.call-start = ((), (), s32[]{:S(2)}) async-start(), calls=%async_computation.1 | async-start | bytes 2359296 | tf_op jit(solution)/shard_map/psum | solution.py:105
  146.3 9.6 %copy-start.4 = (f32[32]{0:T(128)S(1)}, f32[32]{0:T(128)}, u32[]{:S(2)}) copy-start(f32[32]{0:T(128)} %param.8) | copy-start | bytes 388
  146.4 9.6 %copy-start.2 = (s32[64]{0:T(128)S(1)}, s32[64]{0:T(128)}, u32[]{:S(2)}) copy-start(s32[64]{0:T(128)} %param.9) | copy-start | bytes 772
  146.4 9.9 %copy-start.1 = (bf16[64,128]{1,0:T(8,128)(2,1)S(1)}, bf16[64,128]{1,0:T(8,128)(2,1)}, u32[]{:S(2)}) copy-start(bf16[64,128]{1,0:T(8,128)(2,1)} %param.5) | copy-start | bytes 49156
  160.2 4.4 copy-start
  164.6 2.4 copy-start.3
  164.6 3.7 copy-start.5
  166.8 462.2 %all-reduce.8.cloned.1.call-start = ((), (), s32[]{:S(2)}) async-start(), calls=%async_computation.3 | async-start | bytes 3145728
  335.4 380.7 %reduce-scatter.3.cloned.1.call-start = ((), (), s32[]{:S(2)}) async-start(), calls=%async_computation.2 | async-start | bytes 1671168 | tf_op jit(solution)/shard_map/reduce_scatter | solution.py:119
Sparse Core Ops, SparseCore 0:
  166.9 143.9 all-reduce.5
  335.5 293.3 all-reduce.7
  632.1 83.9 reduce-scatter.2
where the time goes:
time: 727 us; the launch traced here: 725 us
  waiting for transfers between devices  395 us (54%)
  blocking collectives  196 us (27%)
  local copies, waits for them, and re-layouts  92.5 us (13%)
  matrix products  20.8 us (3%)
  between operations  15.3 us (2%)
    unnamed x4, waiting for transfers between devices  228 us
    unnamed x2, blocking collectives  123 us
    reduce_scatter x1, waiting for transfers between devices, on_device(): owned = lax.psum_scatter(owned, 'ptcl', scatter_dimension=1, tiled=True)  83.5 us
    psum x1, waiting for transfers between devices, on_device(): summed_scores = lax.psum(partial_scores, 'ptcl')  83.1 us
    all_gather x1, blocking collectives, on_device(): lax.all_gather(references, 'cls', axis=0, tiled=True)  72.3 us
    reshape x2, local copies, waits for them, and re-layouts, on_device(): all_refs.reshape(class_count, pix_count, 2)  31.2 us
    all_gather x1, local copies, waits for them, and re-layouts, on_device(): lax.all_gather(references, 'cls', axis=0, tiled=True)  27 us
  transfers between devices with their start and end apart: 3, of which 3 were waited for; matrix products, arithmetic and copies ran while one was open for 0% of the time, Pallas kernels for 0%

commit v1 on v0

v1 whole, which is shorter than its diff:
```python
import functools
import math

import jax
import jax.numpy as jnp
import numpy as np
from jax import lax
from jax.experimental import pallas as pl
from jax.experimental.pallas import tpu as pltpu
from jax.sharding import PartitionSpec as P

SIDE = 32
PIX = SIDE * SIDE
ROT = 36
BASE = ROT // 4
EXT = SIDE + 1
LANES = 1152
CHUNK = 384
CLS = 32
PTCL = 16
NK = 8
ROWS = BASE * NK
NB = 64
MESH = pl.DeviceIdType.MESH
F32 = jnp.float32
BF16 = jnp.bfloat16
VMEM = pltpu.VMEM


def grid_constants():
    table = np.zeros((16, LANES), np.float32)
    e = np.arange(EXT * EXT)
    across = e % EXT - SIDE // 2
    down = e // EXT - SIDE // 2
    table[0, : e.size] = across
    table[1, : e.size] = down
    table[2, : e.size] = (across * across + down * down) / float((SIDE // 2) ** 2)
    table[4:8] = -1.0
    a, d = across.copy(), down.copy()
    for s in range(4):
        inside = (a >= -16) & (a <= 15) & (d >= -16) & (d <= 15)
        table[4 + s, : e.size] = np.where(inside, (d + 16) * SIDE + a + 16, -1)
        table[8 + s, : e.size] = inside
        a, d = -d, a
    return table


def angle_constants():
    angles = (np.float32(2.0 * math.pi) * np.arange(BASE, dtype=np.float32) / np.float32(ROT)).astype(np.float32)
    return np.stack([np.cos(angles), np.sin(angles)]).astype(np.float32)


def split_constants():
    out = np.zeros((128, 128), np.float32)
    for l in range(64):
        out[2 * l, l] = 1
        out[2 * l + 1, 64 + l] = 1
    return out.astype(jnp.bfloat16)


def join_constants():
    out = np.zeros((2, 256, 128), np.float32)
    for h in range(2):
        for l in range(64):
            out[h, 64 * h + l, 2 * l] = 1
            out[h, 128 + 64 * h + l, 2 * l + 1] = 1
    return out


def sine_of(phase):
    return jnp.sin(phase)


def factors(grid_ref, cosine, sine, start):
    qa = grid_ref[0:1, pl.ds(start, CHUNK)]
    qd = grid_ref[1:2, pl.ds(start, CHUNK)]
    place = lax.broadcasted_iota(jnp.int32, (SIDE, CHUNK), 0).astype(F32) - float(SIDE // 2)
    hat_a = jnp.maximum(0.0, 1.0 - jnp.abs(cosine * qa + sine * qd - place))
    hat_d = jnp.maximum(0.0, 1.0 - jnp.abs(cosine * qd - sine * qa - place))
    return hat_a, hat_d


def table_rows(hat_a, hat_d, first):
    return jnp.concatenate(
        [hat_a * hat_d[first + i : first + i + 1, :] for i in range(8)], axis=0
    ).astype(BF16)


def pair_halves(first, second):
    low = lax.broadcasted_iota(jnp.int32, first.shape, 1) < 64
    real = jnp.where(low, first, pltpu.roll(second, 64, 1))
    imag = jnp.where(low, pltpu.roll(first, 64, 1), second)
    return real, imag


def score_kernel(
    angle_ref, grid_ref, split_ref, imgs_ref, refs_ref, focus_ref,
    logit_ref, stat_ref, vals_ref,
    flat, wide, refmat, turned, power_lo,
):
    flat[0 : NK * 32, :] = jnp.dot(
        refs_ref[...].reshape(NK * 32, 128), split_ref[...], preferred_element_type=F32
    )
    for u in range(8):
        real, imag = pair_halves(
            flat[pl.ds(2 * u, NK, stride=32), :], flat[pl.ds(2 * u + 1, NK, stride=32), :]
        )
        refmat[:, 128 * u : 128 * (u + 1)] = jnp.concatenate([real, imag], axis=0).astype(BF16)
    prior = flat[pl.ds(16, NK, stride=32), :]

    def rotate(step, _):
        r = step // (LANES // CHUNK)
        start = pl.multiple_of((step % (LANES // CHUNK)) * CHUNK, CHUNK)
        hat_a, hat_d = factors(grid_ref, angle_ref[0, r], angle_ref[1, r], start)
        acc = jnp.zeros((2 * NK, CHUNK), F32)
        for part in range(4):
            rows = table_rows(hat_a, hat_d, 8 * part)
            acc += jnp.dot(refmat[:, 256 * part : 256 * (part + 1)], rows, preferred_element_type=F32)
        acc = acc.astype(BF16).astype(F32)
        row = pl.multiple_of(r * NK, NK)
        turned[0, pl.ds(row, NK), pl.ds(start, CHUNK)] = acc[:NK]
        turned[1, pl.ds(row, NK), pl.ds(start, CHUNK)] = acc[NK:]
        return 0

    lax.fori_loop(0, BASE * (LANES // CHUNK), rotate, 0)

    for u in range(8):
        two = jnp.dot(
            imgs_ref[2 * u : 2 * u + 2].reshape(128, 128), split_ref[...], preferred_element_type=F32
        )
        real, imag = pair_halves(two[:NB], two[NB:])
        wide[:, 128 * u : 128 * (u + 1)] = jnp.concatenate([real, imag], axis=0).astype(BF16)

    phase = math.pi * focus_ref[...] * grid_ref[2:3, :]
    contrast = -(0.99499 * jnp.sin(phase) + 0.1 * jnp.cos(phase))
    square = contrast * contrast

    def turn(s, _):
        target = grid_ref[pl.ds(4 + s, 1), :]
        mask = grid_ref[pl.ds(8 + s, 1), :]
        acc = jnp.zeros((2 * NB, LANES), F32)
        for part in range(4):
            place = lax.broadcasted_iota(jnp.int32, (256, LANES), 0).astype(F32) + 256.0 * part
            pick = jnp.where(place == target, 1.0, 0.0).astype(BF16)
            acc += jnp.dot(wide[:, 256 * part : 256 * (part + 1)], pick, preferred_element_type=F32)
        row = pl.multiple_of(s * NB, NB)
        vals_ref[0, pl.ds(row, NB), :] = (acc[:NB] * contrast).astype(BF16)
        vals_ref[1, pl.ds(row, NB), :] = (acc[NB:] * contrast).astype(BF16)
        masked = square * mask
        high = masked.astype(BF16)
        vals_ref[2, pl.ds(row, NB), :] = high
        power_lo[pl.ds(row, NB), :] = (masked - high.astype(F32)).astype(BF16)
        return 0

    lax.fori_loop(0, 4, turn, 0)

    def over_pixels(a, b):
        return lax.dot_general(a, b, (((1,), (1,)), ((), ())), preferred_element_type=F32)

    real, imag = turned[0], turned[1]
    match = over_pixels(real.astype(BF16), vals_ref[0]) + over_pixels(imag.astype(BF16), vals_ref[1])
    power = real * real + imag * imag
    power_high = power.astype(BF16)
    power_low = (power - power_high.astype(F32)).astype(BF16)
    penalty = (
        over_pixels(power_high, vals_ref[2])
        + over_pixels(power_low, vals_ref[2])
        + over_pixels(power_high, power_lo[...])
    )
    both = jnp.concatenate([prior, prior], axis=1)
    logits = match - 0.5 * penalty + jnp.concatenate([both] * BASE, axis=0)
    logit_ref[...] = logits
    peak = jnp.max(logits, axis=0, keepdims=True)
    peak = jnp.maximum(peak[:, :128], peak[:, 128:])
    peak = jnp.maximum(peak, pltpu.roll(peak, 64, 1))
    total = jnp.sum(jnp.exp(logits - jnp.concatenate([peak, peak], axis=1)), axis=0, keepdims=True)
    total = total[:, :128] + total[:, 128:]
    total = total + pltpu.roll(total, 64, 1)
    stat_ref[...] = jnp.where(lax.broadcasted_iota(jnp.int32, (8, 128), 0) == 0, peak, total)


def score(imgs, refs, focus):
    vmem = pl.BlockSpec(memory_space=VMEM)
    return pl.pallas_call(
        score_kernel,
        out_shape=(
            jax.ShapeDtypeStruct((ROWS, 4 * NB), F32),
            jax.ShapeDtypeStruct((8, 128), F32),
            jax.ShapeDtypeStruct((3, 4 * NB, LANES), BF16),
        ),
        in_specs=[pl.BlockSpec(memory_space=pltpu.SMEM)] + [vmem] * 5,
        out_specs=(vmem, vmem, vmem),
        scratch_shapes=[
            VMEM((NK * 32, 128), F32),
            VMEM((2 * NB, PIX), BF16),
            VMEM((2 * NK, PIX), BF16),
            VMEM((2, ROWS, LANES), F32),
            VMEM((4 * NB, LANES), BF16),
        ],
        compiler_params=pltpu.CompilerParams(vmem_limit_bytes=48 << 20),
        name="score",
    )(jnp.asarray(angle_constants()), jnp.asarray(grid_constants()), jnp.asarray(split_constants()), imgs, refs, focus)


def sums_kernel(angle_ref, grid_ref, logit_ref, stats_ref, vals_ref, out_ref, spread, acc):
    peaks = stats_ref[:, 0:1, :]
    peak = jnp.max(peaks, axis=0)
    total = jnp.sum(stats_ref[:, 1:2, :] * jnp.exp(peaks - peak[None]), axis=0)
    peak2 = jnp.concatenate([peak, peak], axis=1)
    total2 = jnp.concatenate([total, total], axis=1)
    weights = (jnp.exp(logit_ref[...] - peak2) / total2).astype(BF16)
    counts = jnp.sum(weights.astype(F32), axis=1, keepdims=True)
    share = counts[0:NK]
    for r in range(1, BASE):
        share = share + counts[r * NK : (r + 1) * NK]
    for c in range(3):
        spread[c] = jnp.dot(weights, vals_ref[c], preferred_element_type=F32)
    acc[...] = jnp.zeros_like(acc)

    def project(step, _):
        r = step // (LANES // CHUNK)
        start = pl.multiple_of((step % (LANES // CHUNK)) * CHUNK, CHUNK)
        hat_a, hat_d = factors(grid_ref, angle_ref[0, r], angle_ref[1, r], start)
        row = pl.multiple_of(r * NK, NK)
        parts = jnp.concatenate([spread[c, pl.ds(row, NK), pl.ds(start, CHUNK)] for c in range(3)], axis=0)
        high = parts.astype(BF16)
        low = (parts - high.astype(F32)).astype(BF16)
        both = jnp.concatenate([high.astype(F32), low.astype(F32)], axis=0).astype(BF16)
        for part in range(4):
            rows = table_rows(hat_a, hat_d, 8 * part)
            acc[:, 256 * part : 256 * (part + 1)] += lax.dot_general(
                both, rows, (((1,), (1,)), ((), ())), preferred_element_type=F32
            )
        return 0

    lax.fori_loop(0, BASE * (LANES // CHUNK), project, 0)
    back = acc[0:24, :] + acc[24:48, :]
    for k in range(NK):
        for c in range(3):
            for u in range(8):
                out_ref[k, 8 * c + u : 8 * c + u + 1, :] = back[
                    NK * c + k : NK * c + k + 1, 128 * u : 128 * (u + 1)
                ]
        out_ref[k, 24:32, :] = jnp.broadcast_to(share[k : k + 1, :], (8, 128))


def sums(logits, stats, vals):
    vmem = pl.BlockSpec(memory_space=VMEM)
    return pl.pallas_call(
        sums_kernel,
        out_shape=jax.ShapeDtypeStruct((NK, 32, 128), F32),
        in_specs=[pl.BlockSpec(memory_space=pltpu.SMEM)] + [vmem] * 4,
        out_specs=vmem,
        scratch_shapes=[VMEM((3, ROWS, LANES), F32), VMEM((48, PIX), F32)],
        compiler_params=pltpu.CompilerParams(vmem_limit_bytes=48 << 20),
        name="sums",
    )(jnp.asarray(angle_constants()), jnp.asarray(grid_constants()), logits, stats, vals)


def gather_kernel(img_ref, msg_ref, imgs_ref, refs_ref, send, recv, rsend, rrecv):
    c = lax.axis_index("cls")
    j = lax.axis_index("ptcl")
    home = j // 4
    sender = lax.rem(c, 4) == home
    barrier = pltpu.get_barrier_semaphore()

    def greet_row(d, _):
        pl.semaphore_signal(barrier, inc=1, device_id={"ptcl": lax.rem(j + d, PTCL)}, device_id_type=MESH)
        return 0

    lax.fori_loop(1, PTCL, greet_row, 0)

    def greet_column(g, _):
        @pl.when(4 * g + home != c)
        def _():
            pl.semaphore_signal(barrier, inc=1, device_id={"cls": 4 * g + home}, device_id_type=MESH)

        return 0

    lax.fori_loop(0, NK, greet_column, 0)
    @pl.when(sender)
    def _():
        pl.semaphore_wait(barrier, PTCL - 1 + CLS - 1)

    @pl.when(jnp.logical_not(sender))
    def _():
        pl.semaphore_wait(barrier, PTCL - 1)

    def image(d):
        return pltpu.make_async_remote_copy(
            src_ref=img_ref, dst_ref=imgs_ref.at[j], send_sem=send.at[d], recv_sem=recv.at[d],
            device_id={"ptcl": lax.rem(j + d, PTCL)}, device_id_type=MESH,
        )

    def ref_row(d):
        return pltpu.make_async_remote_copy(
            src_ref=msg_ref.at[lax.rem(j, 4)], dst_ref=refs_ref.at[c // 4], send_sem=rsend.at[d],
            recv_sem=rrecv.at[c // 4], device_id={"cls": lax.rem(c + d, CLS)}, device_id_type=MESH,
        )

    def ref_arrival(g):
        return pltpu.make_async_remote_copy(
            src_ref=msg_ref.at[0], dst_ref=refs_ref.at[g], send_sem=rsend.at[0],
            recv_sem=rrecv.at[g], device_id={"cls": lax.rem(c + 1, CLS)}, device_id_type=MESH,
        )

    @pl.when(sender)
    def _():
        def start_ref(d, _):
            ref_row(d).start()
            return 0

        lax.fori_loop(1, CLS, start_ref, 0)

    def start_image(d, _):
        image(d).start()
        return 0

    lax.fori_loop(1, PTCL, start_image, 0)
    imgs_ref[j] = img_ref[...]

    @pl.when(sender)
    def _():
        refs_ref[c // 4] = msg_ref[lax.rem(j, 4)]

    def arrive_image(d, _):
        pltpu.make_async_remote_copy(
            src_ref=img_ref, dst_ref=imgs_ref.at[lax.rem(j + PTCL - d, PTCL)], send_sem=send.at[d],
            recv_sem=recv.at[d], device_id={"ptcl": lax.rem(j + d, PTCL)}, device_id_type=MESH,
        ).wait_recv()
        return 0

    lax.fori_loop(1, PTCL, arrive_image, 0)

    def arrive_ref(g, _):
        @pl.when(4 * g + home != c)
        def _():
            ref_arrival(g).wait_recv()

        return 0

    lax.fori_loop(0, NK, arrive_ref, 0)

    def leave_image(d, _):
        image(d).wait_send()
        return 0

    lax.fori_loop(1, PTCL, leave_image, 0)

    @pl.when(sender)
    def _():
        def leave_ref(d, _):
            ref_row(d).wait_send()
            return 0

        lax.fori_loop(1, CLS, leave_ref, 0)


def gather(image, message):
    vmem = pl.BlockSpec(memory_space=VMEM)
    return pl.pallas_call(
        gather_kernel,
        out_shape=(
            jax.ShapeDtypeStruct((PTCL, NB, 128), BF16),
            jax.ShapeDtypeStruct((NK, 32, 128), BF16),
        ),
        in_specs=[vmem, vmem],
        out_specs=(vmem, vmem),
        scratch_shapes=[
            pltpu.SemaphoreType.DMA((PTCL,)),
            pltpu.SemaphoreType.DMA((PTCL,)),
            pltpu.SemaphoreType.DMA((CLS,)),
            pltpu.SemaphoreType.DMA((NK,)),
        ],
        compiler_params=pltpu.CompilerParams(collective_id=0, has_side_effects=True),
        name="gather",
    )(image, message)


def stats_kernel(stat_ref, stats_ref, send, recv):
    j = lax.axis_index("ptcl")
    barrier = pltpu.get_barrier_semaphore()

    def greet(d, _):
        pl.semaphore_signal(barrier, inc=1, device_id={"ptcl": lax.rem(j + d, PTCL)}, device_id_type=MESH)
        return 0

    lax.fori_loop(1, PTCL, greet, 0)
    pl.semaphore_wait(barrier, PTCL - 1)

    def copy(d, slot):
        return pltpu.make_async_remote_copy(
            src_ref=stat_ref, dst_ref=stats_ref.at[slot], send_sem=send.at[d], recv_sem=recv.at[d],
            device_id={"ptcl": lax.rem(j + d, PTCL)}, device_id_type=MESH,
        )

    def start(d, _):
        copy(d, j).start()
        return 0

    lax.fori_loop(1, PTCL, start, 0)
    stats_ref[j] = stat_ref[...]

    def finish(d, _):
        copy(d, lax.rem(j + PTCL - d, PTCL)).wait_recv()
        copy(d, j).wait_send()
        return 0

    lax.fori_loop(1, PTCL, finish, 0)


def exchange(stat):
    vmem = pl.BlockSpec(memory_space=VMEM)
    return pl.pallas_call(
        stats_kernel,
        out_shape=jax.ShapeDtypeStruct((PTCL, 8, 128), F32),
        in_specs=[vmem],
        out_specs=vmem,
        scratch_shapes=[pltpu.SemaphoreType.DMA((PTCL,)), pltpu.SemaphoreType.DMA((PTCL,))],
        compiler_params=pltpu.CompilerParams(collective_id=1, has_side_effects=True),
        name="exchange",
    )(stat)


def finish_kernel(join_ref, part_ref, new_ref, share_ref, heap, outbox, inbox, s1, r1, s2, r2):
    c = lax.axis_index("cls")
    j = lax.axis_index("ptcl")
    home = j // 4
    mine = c // 4
    owner = lax.rem(c, 4) == home
    first = 4 * lax.rem(c, 4)
    barrier = pltpu.get_barrier_semaphore()

    @pl.when(owner)
    def _():
        def greet(d, _):
            pl.semaphore_signal(barrier, inc=1, device_id={"cls": lax.rem(c + d, CLS)}, device_id_type=MESH)
            return 0

        lax.fori_loop(1, CLS, greet, 0)

    def greet_owner(i, _):
        @pl.when(first + i != j)
        def _():
            pl.semaphore_signal(barrier, inc=1, device_id={"ptcl": first + i}, device_id_type=MESH)

        return 0

    lax.fori_loop(0, 4, greet_owner, 0)

    @pl.when(owner)
    def _():
        pl.semaphore_wait(barrier, NK - 1 + PTCL - 1)

    @pl.when(jnp.logical_not(owner))
    def _():
        pl.semaphore_wait(barrier, NK)

    def to_owner(g):
        return pltpu.make_async_remote_copy(
            src_ref=part_ref.at[g], dst_ref=heap.at[c], send_sem=s1.at[g], recv_sem=r1.at[c],
            device_id={"cls": 4 * g + home}, device_id_type=MESH,
        )

    def start_sum(g, _):
        @pl.when(4 * g + home != c)
        def _():
            to_owner(g).start()

        return 0

    lax.fori_loop(0, NK, start_sum, 0)

    def to_row(d):
        target = lax.rem(j + d, PTCL)
        return pltpu.make_async_remote_copy(
            src_ref=outbox.at[target], dst_ref=inbox.at[lax.rem(j, 4)], send_sem=s2.at[d],
            recv_sem=r2.at[lax.rem(j, 4)], device_id={"ptcl": target}, device_id_type=MESH,
        )

    @pl.when(owner)
    def _():
        heap[c] = part_ref[mine]

        def arrive(d, _):
            source = lax.rem(c + d, CLS)
            pltpu.make_async_remote_copy(
                src_ref=part_ref.at[0], dst_ref=heap.at[source], send_sem=s1.at[0], recv_sem=r1.at[source],
                device_id={"cls": source}, device_id_type=MESH,
            ).wait_recv()
            return 0

        lax.fori_loop(1, CLS, arrive, 0)
        total = lax.fori_loop(1, CLS, lambda i, t: t + heap[i], heap[0])
        scale = 1.0 / (total[16:24] + 1.0)
        planes = jnp.concatenate([total[0:8] * scale, total[8:16] * scale], axis=1)
        row = lax.broadcasted_iota(jnp.int32, (8, 128), 0)
        for h in range(2):
            joined = jnp.dot(planes, join_ref[h], precision=lax.Precision.HIGHEST, preferred_element_type=F32)
            for u in range(8):
                outbox[2 * u + h] = jnp.where(row == 0, joined[u : u + 1, :], total[24:25, :])

        def start_row(d, _):
            to_row(d).start()
            return 0

        lax.fori_loop(1, PTCL, start_row, 0)
        inbox[lax.rem(j, 4)] = outbox[j]

    def arrive_row(i, _):
        @pl.when(first + i != j)
        def _():
            pltpu.make_async_remote_copy(
                src_ref=outbox.at[0], dst_ref=inbox.at[i], send_sem=s2.at[0], recv_sem=r2.at[i],
                device_id={"ptcl": lax.rem(j + 1, PTCL)}, device_id_type=MESH,
            ).wait_recv()

        return 0

    lax.fori_loop(0, 4, arrive_row, 0)
    new_ref[...] = jnp.concatenate([inbox[i, 0:1, :] for i in range(4)], axis=0)
    share_ref[...] = jnp.concatenate([inbox[i, 1:2, :] for i in range(4)], axis=0)

    def leave_sum(g, _):
        @pl.when(4 * g + home != c)
        def _():
            to_owner(g).wait_send()

        return 0

    lax.fori_loop(0, NK, leave_sum, 0)

    @pl.when(owner)
    def _():
        def leave_row(d, _):
            to_row(d).wait_send()
            return 0

        lax.fori_loop(1, PTCL, leave_row, 0)


def finish(parts):
    vmem = pl.BlockSpec(memory_space=VMEM)
    return pl.pallas_call(
        finish_kernel,
        out_shape=(jax.ShapeDtypeStruct((4, 128), F32), jax.ShapeDtypeStruct((4, 128), F32)),
        in_specs=[vmem, vmem],
        out_specs=(vmem, vmem),
        scratch_shapes=[
            VMEM((CLS, 32, 128), F32),
            VMEM((PTCL, 8, 128), F32),
            VMEM((4, 8, 128), F32),
            pltpu.SemaphoreType.DMA((NK,)),
            pltpu.SemaphoreType.DMA((CLS,)),
            pltpu.SemaphoreType.DMA((PTCL,)),
            pltpu.SemaphoreType.DMA((4,)),
        ],
        compiler_params=pltpu.CompilerParams(collective_id=2, has_side_effects=True),
        name="finish",
    )(jnp.asarray(join_constants()), parts)


def on_device(images, references, log_prior, defocus, groups):
    prior = jnp.broadcast_to(log_prior[:, None, None], (4, 16, 128))
    message = jnp.concatenate([references.reshape(4, 16, 128), prior], axis=1)
    imgs, refs = gather(images, message)
    pick = groups[:, None] == jnp.arange(defocus.shape[0], dtype=jnp.int32)[None, :]
    focus = jnp.sum(jnp.where(pick, defocus[None, :], 0.0), axis=1, keepdims=True)
    logits, stat, vals = score(imgs, refs, focus)
    parts = sums(logits, exchange(stat), vals)
    new, share = finish(parts)
    return new, share[:, 0] * (128.0 / 2048.0)


def solution(mesh):
    return jax.shard_map(
        on_device,
        mesh=mesh,
        in_specs=(P("cls", "ptcl"), P("cls", None), P("cls"), P(), P("cls")),
        out_specs=(P("cls", "ptcl"), P("cls")),
        check_vma=False,
    )
```

time: 727 us -> 101 us (0.14)
  waiting for transfers between devices: 395 us -> 0 us
  blocking collectives: 196 us -> 0 us
  Pallas kernels: 0 us -> 86.9 us
  local copies, waits for them, and re-layouts: 92.5 us -> 10.5 us
  matrix products: 20.8 us -> 0 us
  between operations: 15.3 us -> 0.7 us
    unnamed x4 -> x0, waiting for transfers between devices: 228 us -> none
    unnamed x2 -> x0, blocking collectives: 123 us -> none
    pallas_call x0 -> x5, Pallas kernels: none -> 86.9 us  [the longest x1 25.9 us: gather(): pl.pallas_call(gather_kernel, out_shape=(jax.ShapeDtypeStruct((PTCL, NB,...]
    reduce_scatter x1 -> x0, waiting for transfers between devices: 83.5 us -> none  [on_device(): owned = lax.psum_scatter(owned, 'ptcl', scatter_dimension=1, tiled=True)]
    psum x1 -> x0, waiting for transfers between devices: 83.1 us -> none  [on_device(): summed_scores = lax.psum(partial_scores, 'ptcl')]
    all_gather x1 -> x0, blocking collectives: 72.3 us -> none  [on_device(): lax.all_gather(references, 'cls', axis=0, tiled=True)]
    reshape x7 -> x0, local copies, waits for them, and re-layouts: 44.1 us -> none  [the longest x2 31.2 us: on_device(): all_refs.reshape(class_count, pix_count, 2)]
    all_gather x1 -> x0, local copies, waits for them, and re-layouts: 27 us -> none  [on_device(): lax.all_gather(references, 'cls', axis=0, tiled=True)]
  transfers between devices with their start and end apart: 3 -> 0, of which waited for: 3 -> 0; matrix products, arithmetic and copies ran while one was open for 0% -> 0% of each run, Pallas kernels for 0% -> 0%
where the time goes in v1:
time: 101 us
  Pallas kernels  86.9 us (86%)
  local copies, waits for them, and re-layouts  10.5 us (10%)
  other arithmetic  2.66 us (3%)
    pallas_call x1, Pallas kernels, gather(): pl.pallas_call(gather_kernel, out_shape=(jax.ShapeDtypeStruct((PTCL, NB,...  25.9 us
    pallas_call x1, Pallas kernels, finish(): pl.pallas_call(finish_kernel, out_shape=(jax.ShapeDtypeStruct((4, 128), F...  25.4 us
    pallas_call x1, Pallas kernels, exchange(): pl.pallas_call(stats_kernel, out_shape=jax.ShapeDtypeStruct((PTCL, 8, 128...  12.2 us
    pallas_call x1, Pallas kernels, score(): pl.pallas_call(score_kernel, out_shape=(jax.ShapeDtypeStruct((ROWS, 4 * N...  12.1 us
    pallas_call x1, Pallas kernels, sums(): pl.pallas_call(sums_kernel, out_shape=jax.ShapeDtypeStruct((NK, 32, 128),...  11.3 us
    unnamed x22, local copies, waits for them, and re-layouts  9.7 us

profile of v1, /device:TPU:1, one launch (start us, length us, event | category | flops | bytes accessed | tf_op | source)
XLA Modules:
  0.0 100.8 jit_solution(10724822917732982190)
XLA Ops:
  0.6 0.8 select_reduce_fusion
  1.4 0.7 copy.18
  2.1 0.7 broadcast_in_dim.24
  2.8 0.6 pad_maximum_fusion.msg_ref
  3.4 0.1 copy.15.focus_ref
  3.5 25.9 %gather.1 = (bf16[16,64,128]{2,1,0:T(8,128)(2,1)}, bf16[8,32,128]{2,1,0:T(8,128)(2,1)}) custom-call(bf16[64,128]{1,0:T(8,128)(2,1)} %img_ref.1, bf16[4,32,128]{2,1,0:T(8,128)(2,1)} %pad_maximum_fusion.msg_ref), custom_call_target="tpu_custom_call" | custom-call | tf_op jit(solution)/shard_map/gather/pallas_call | solution.py:361
  29.4 0.0 copy-start.1
  29.4 0.9 copy-done.1
  30.3 0.0 copy-start.3
  30.3 0.9 copy-done.3
  31.3 0.0 copy-start.5
  31.3 0.8 copy-done.5
  32.1 0.0 copy-start.6
  32.1 0.8 copy-done.6
  32.8 0.0 copy-start.7
  32.9 0.7 copy-done.7
  33.5 12.1 %score.1 = (f32[72,256]{1,0:T(8,128)S(1)}, f32[8,128]{1,0:T(8,128)S(1)}, bf16[3,256,1152]{2,1,0:T(8,128)(2,1)S(1)}) custom-call(f32[2,9]{1,0:T(2,128)S(1)} %copy-done.7, f32[16,1152]{1,0:T(8,128)S(1)} %copy-done.1, bf16[128,128]{1,0:T(8,128)(2,1)S(1)} %copy-done.6, bf16[16,64,128]{2,1,0:T(8,128)(2,1)S(1)} %copy-done.3, bf16[8,32,128]{2,1,0:T(8,128)(2,1)S(1)} %copy-done.5, ...), custom_call_target="tpu_custom_call" | custom-call | tf_op jit(solution)/shard_map/score/pallas_call | solution.py:184
  45.7 0.0 copy-start.9
  45.7 0.6 copy-done.9
  46.3 12.2 %exchange.1.stats_ref = f32[16,8,128]{2,1,0:T(8,128)} custom-call(f32[8,128]{1,0:T(8,128)} %copy-done.9), custom_call_target="tpu_custom_call" | custom-call | tf_op jit(solution)/shard_map/exchange/pallas_call | solution.py:414
  58.5 0.0 copy-start.2
  58.5 0.9 copy-done.2
  59.4 0.0 copy-start.4
  59.4 0.8 copy-done.4
  60.2 0.0 copy-start.8
  60.2 0.7 copy-done.8
  60.9 11.3 %sums.1.part_ref = f32[8,32,128]{2,1,0:T(8,128)S(1)} custom-call(f32[2,9]{1,0:T(2,128)S(1)} %copy-done.8, f32[16,1152]{1,0:T(8,128)S(1)} %copy-done.2, f32[72,256]{1,0:T(8,128)S(1)} %get-tuple-element.11.logit_ref, f32[16,8,128]{2,1,0:T(8,128)S(1)} %copy-done.4, bf16[3,256,1152]{2,1,0:T(8,128)(2,1)S(1)} %get-tuple-element.13.vals_ref), custom_call_target="tpu_custom_call" | custom-call | tf_op jit(solution)/shard_map/sums/pallas_call | solution.py:249
  72.2 0.0 copy-start
  72.2 0.6 copy-done
  72.9 25.4 %finish.1 = (f32[4,128]{1,0:T(4,128)}, f32[4,128]{1,0:T(4,128)}) custom-call(f32[2,256,128]{2,1,0:T(8,128)} %constant.15.clone.join_ref, f32[8,32,128]{2,1,0:T(8,128)} %copy-done), custom_call_target="tpu_custom_call" | custom-call | tf_op jit(solution)/shard_map/finish/pallas_call | solution.py:544
  98.2 1.3 %multiply_reduce_fusion = f32[4]{0:T(128)} fusion(f32[4,128]{1,0:T(4,128)} %get-tuple-element.15), kind=kLoop, calls=%fused_computation.4 | loop fusion | flops 4 | bytes 32 | tf_op jit(solution)/shard_map/mul | solution.py:572
  99.5 1.2 %copy.20 = f32[4,128]{1,0:T(4,128)} copy(f32[4,128]{1,0:T(4,128)} %get-tuple-element.18) | data formatting | bytes 4096
Async XLA Ops:
  29.4 0.9 copy-start.1
  30.3 0.9 copy-start.3
  31.3 0.8 copy-start.5
  32.1 0.8 copy-start.6
  32.8 0.7 copy-start.7
  45.7 0.6 copy-start.9
  58.5 0.9 copy-start.2
  59.4 0.8 copy-start.4
  60.2 0.7 copy-start.8
  72.2 0.7 copy-start

commit v2 on v0

v2 whole, which is shorter than its diff:
```python
import functools
import math

import jax
import jax.numpy as jnp
import numpy as np
from jax import lax
from jax.experimental import pallas as pl
from jax.experimental.pallas import tpu as pltpu
from jax.sharding import PartitionSpec as P

SIDE = 32
PIX = SIDE * SIDE
ROT = 36
BASE = ROT // 4
EXT = SIDE + 1
LANES = 1152
CHUNK = 384
CLS = 32
PTCL = 16
NK = 8
ROWS = BASE * NK
NB = 64
MESH = pl.DeviceIdType.MESH
F32 = jnp.float32
BF16 = jnp.bfloat16
VMEM = pltpu.VMEM

ANGLES = (np.float32(2.0 * math.pi) * np.arange(BASE, dtype=np.float32) / np.float32(ROT)).astype(np.float32)
COSINES = [float(x) for x in np.cos(ANGLES).astype(np.float32)]
SINES = [float(x) for x in np.sin(ANGLES).astype(np.float32)]


def choose(values, r):
    out = jnp.float32(values[0])
    for i, value in enumerate(values[1:], 1):
        out = jnp.where(r == i, jnp.float32(value), out)
    return out


def iota(shape, axis):
    return lax.broadcasted_iota(jnp.int32, shape, axis)


def grid_rows(grid):
    e = iota((1, LANES), 1).astype(F32)
    down = jnp.floor((e + 0.5) * (1.0 / EXT))
    across = e - EXT * down - SIDE // 2
    down = down - SIDE // 2
    grid[0:1, :] = across
    grid[1:2, :] = down
    grid[2:3, :] = (across * across + down * down) * (1.0 / (SIDE // 2) ** 2)
    a, d = across, down
    for s in range(4):
        inside = (a >= -16.0) & (a <= 15.0) & (d >= -16.0) & (d <= 15.0)
        grid[4 + s : 5 + s, :] = jnp.where(inside, (d + 16.0) * SIDE + a + 16.0, -1.0)
        a, d = -d, a


def split_matrix():
    source, place = iota((128, 128), 0), iota((128, 128), 1)
    return jnp.where(source == 2 * (place % 64) + place // 64, 1.0, 0.0).astype(BF16)


def join_matrix():
    source, place = iota((256, 256), 0), iota((256, 256), 1)
    inner = place % 128
    return jnp.where(source == 128 * (inner % 2) + 64 * (place // 128) + inner // 2, 1.0, 0.0).astype(BF16)


def pair_halves(first, second):
    low = iota(first.shape, 1) < 64
    real = jnp.where(low, first, pltpu.roll(second, 64, 1))
    imag = jnp.where(low, pltpu.roll(first, 64, 1), second)
    return real, imag


def column_of(row, size):
    return jnp.sum(jnp.where(iota((size, size), 0) == iota((size, size), 1), row, 0.0), axis=1, keepdims=True)


def over_lanes(a, b):
    return lax.dot_general(a, b, (((1,), (1,)), ((), ())), preferred_element_type=F32)


def make_tables(grid, tables):
    def step(i, _):
        r = i // (LANES // CHUNK)
        start = pl.multiple_of((i % (LANES // CHUNK)) * CHUNK, CHUNK)
        cosine, sine = choose(COSINES, r), choose(SINES, r)
        qa = grid[0:1, pl.ds(start, CHUNK)]
        qd = grid[1:2, pl.ds(start, CHUNK)]
        place = iota((SIDE, CHUNK), 0).astype(F32) - float(SIDE // 2)
        hat_a = jnp.maximum(0.0, 1.0 - jnp.abs(cosine * qa + sine * qd - place))
        hat_d = jnp.maximum(0.0, 1.0 - jnp.abs(cosine * qd - sine * qa - place))
        row = pl.multiple_of(r * PIX, PIX)
        for p in range(SIDE):
            tables[pl.ds(row + p * SIDE, SIDE), pl.ds(start, CHUNK)] = (hat_a * hat_d[p : p + 1, :]).astype(BF16)
        return 0

    lax.fori_loop(0, BASE * (LANES // CHUNK), step, 0)


def make_picks(grid, picks):
    def step(i, _):
        target = grid[pl.ds(4 + i // 4, 1), :]
        place = (iota((256, LANES), 0) + 256 * (i % 4)).astype(F32)
        picks[pl.ds(pl.multiple_of(i * 256, 256), 256), :] = jnp.where(place == target, 1.0, 0.0).astype(BF16)
        return 0

    lax.fori_loop(0, 16, step, 0)


def em_kernel(
    img_ref, ref_ref, prior_ref, focus_ref, group_ref,
    new_ref, share_ref,
    grid, tables, picks, contrast, mrow, message, imgs, refs, flat, wide, refmat, turned, vals, square_lo,
    stat, stats, spread, acc, prow, parts, heap, outbox, inbox,
    img_send, img_recv, ref_send, ref_recv, stat_send, stat_recv, sum_send, sum_recv, out_send, out_recv,
):
    c = lax.axis_index("cls")
    j = lax.axis_index("ptcl")
    home = j // 4
    mine = c // 4
    lane = lax.rem(j, 4)
    owner = lax.rem(c, 4) == home
    first = 4 * lax.rem(c, 4)

    def loop(low, high, body):
        def step(i, _):
            body(i)
            return 0

        lax.fori_loop(low, high, step, 0)

    def owners(body):
        @functools.partial(loop, 0, NK)
        def _(g):
            @pl.when(4 * g + home != c)
            def _():
                body(g)

    def row_peer(d):
        return {"ptcl": lax.rem(j + d, PTCL)}

    def column_peer(d):
        return {"cls": lax.rem(c + d, CLS)}

    def remote(src, dst, send, recv, device):
        return pltpu.make_async_remote_copy(
            src_ref=src, dst_ref=dst, send_sem=send, recv_sem=recv, device_id=device, device_id_type=MESH
        )

    barrier = pltpu.get_barrier_semaphore()

    @pl.when(owner)
    def _():
        loop(1, CLS, lambda d: pl.semaphore_signal(barrier, inc=1, device_id=column_peer(d), device_id_type=MESH))

    @pl.when(jnp.logical_not(owner))
    def _():
        loop(0, NK, lambda g: pl.semaphore_signal(
            barrier, inc=1, device_id={"cls": 4 * g + home}, device_id_type=MESH))

    loop(1, PTCL, lambda d: pl.semaphore_signal(barrier, inc=1, device_id=row_peer(d), device_id_type=MESH))

    split = split_matrix()
    chosen = jnp.sum(
        jnp.where(iota((4, 2 * PIX), 0) == lane, ref_ref[...].astype(F32), 0.0), axis=0, keepdims=True
    )
    for m in range(16):
        mrow[m : m + 1, :] = chosen[:, 128 * m : 128 * (m + 1)]
    own_prior = jnp.sum(jnp.where(iota((1, 4), 1) == lane, prior_ref[...].astype(F32), 0.0), axis=1, keepdims=True)
    mrow[16:32, :] = jnp.broadcast_to(own_prior, (16, 128))
    message[...] = mrow[...].astype(BF16)
    grid_rows(grid)
    group = column_of(group_ref[...].astype(F32), NB)
    groups_count = focus_ref.shape[1]
    focus = jnp.sum(
        jnp.where(group == iota((NB, groups_count), 1).astype(F32), focus_ref[...], 0.0), axis=1, keepdims=True
    )
    phase = math.pi * focus * grid[2:3, :]
    contrast[...] = -(0.99499 * jnp.sin(phase) + 0.1 * jnp.cos(phase))
    make_tables(grid, tables)
    make_picks(grid, picks)

    @pl.when(owner)
    def _():
        pl.semaphore_wait(barrier, PTCL - 1 + CLS - 1)

    @pl.when(jnp.logical_not(owner))
    def _():
        pl.semaphore_wait(barrier, PTCL - 1 + NK)

    def ref_copy(d):
        return remote(message, refs.at[mine], ref_send.at[d], ref_recv.at[mine], column_peer(d))

    def image_copy(d, slot):
        return remote(img_ref, imgs.at[slot], img_send.at[d], img_recv.at[d], row_peer(d))

    @pl.when(owner)
    def _():
        loop(1, CLS, lambda d: ref_copy(d).start())
        refs[mine] = message[...]

    loop(1, PTCL, lambda d: image_copy(d, j).start())
    imgs[j] = img_ref[...]
    loop(1, PTCL, lambda d: image_copy(d, lax.rem(j + PTCL - d, PTCL)).wait_recv())

    for u in range(8):
        two = jnp.dot(imgs[2 * u : 2 * u + 2].reshape(128, 128), split, preferred_element_type=F32)
        real, imag = pair_halves(two[:NB], two[NB:])
        wide[:, 128 * u : 128 * (u + 1)] = jnp.concatenate([real, imag], axis=0).astype(BF16)

    @functools.partial(loop, 0, 4)
    def _(s):
        value = jnp.dot(
            wide[...], picks[pl.ds(pl.multiple_of(s * PIX, PIX), PIX), :], preferred_element_type=F32
        )
        here = contrast[...]
        row = pl.multiple_of(s * NB, NB)
        vals[0, pl.ds(row, NB), :] = (value[:NB] * here).astype(BF16)
        vals[1, pl.ds(row, NB), :] = (value[NB:] * here).astype(BF16)
        square = jnp.where(grid[pl.ds(4 + s, 1), :] >= 0.0, here * here, 0.0)
        high = square.astype(BF16)
        vals[2, pl.ds(row, NB), :] = high
        square_lo[pl.ds(row, NB), :] = (square - high.astype(F32)).astype(BF16)

    owners(lambda g: remote(message, refs.at[g], ref_send.at[0], ref_recv.at[g], column_peer(1)).wait_recv())

    flat[...] = jnp.dot(refs[...].reshape(NK * 32, 128), split, preferred_element_type=F32)
    for u in range(8):
        real, imag = pair_halves(
            flat[pl.ds(2 * u, NK, stride=32), :], flat[pl.ds(2 * u + 1, NK, stride=32), :]
        )
        refmat[:, 128 * u : 128 * (u + 1)] = jnp.concatenate([real, imag], axis=0).astype(BF16)
    prior = flat[pl.ds(16, NK, stride=32), :]

    @functools.partial(loop, 0, BASE)
    def _(r):
        both = jnp.dot(
            refmat[...], tables[pl.ds(pl.multiple_of(r * PIX, PIX), PIX), :], preferred_element_type=F32
        )
        both = both.astype(BF16).astype(F32)
        row = pl.multiple_of(r * NK, NK)
        turned[0, pl.ds(row, NK), :] = both[:NK]
        turned[1, pl.ds(row, NK), :] = both[NK:]

    real, imag = turned[0], turned[1]
    match = over_lanes(real.astype(BF16), vals[0]) + over_lanes(imag.astype(BF16), vals[1])
    power = real * real + imag * imag
    power_hi = power.astype(BF16)
    power_lo = (power - power_hi.astype(F32)).astype(BF16)
    penalty = (
        over_lanes(power_hi, vals[2]) + over_lanes(power_lo, vals[2]) + over_lanes(power_hi, square_lo[...])
    )
    prior = jnp.concatenate([prior, prior], axis=1)
    logits = match - 0.5 * penalty + jnp.concatenate([prior] * BASE, axis=0)
    peak = jnp.max(logits, axis=0, keepdims=True)
    peak = jnp.maximum(peak[:, :128], peak[:, 128:])
    peak = jnp.maximum(peak, pltpu.roll(peak, 64, 1))
    total = jnp.sum(jnp.exp(logits - jnp.concatenate([peak, peak], axis=1)), axis=0, keepdims=True)
    total = total[:, :128] + total[:, 128:]
    total = total + pltpu.roll(total, 64, 1)
    stat[...] = jnp.where(iota((8, 128), 0) == 0, peak, total)

    def stat_copy(d, slot):
        return remote(stat, stats.at[slot], stat_send.at[d], stat_recv.at[d], row_peer(d))

    loop(1, PTCL, lambda d: stat_copy(d, j).start())
    stats[j] = stat[...]
    loop(1, PTCL, lambda d: stat_copy(d, lax.rem(j + PTCL - d, PTCL)).wait_recv())
    peaks = stats[:, 0:1, :]
    peak = jnp.max(peaks, axis=0)
    total = jnp.sum(stats[:, 1:2, :] * jnp.exp(peaks - peak[None]), axis=0)
    weights = (
        jnp.exp(logits - jnp.concatenate([peak, peak], axis=1)) / jnp.concatenate([total, total], axis=1)
    ).astype(BF16)
    counts = jnp.sum(weights.astype(F32), axis=1, keepdims=True)
    share = counts[0:NK]
    for r in range(1, BASE):
        share = share + counts[r * NK : (r + 1) * NK]

    for part in range(3):
        spread[part] = jnp.dot(weights, vals[part], preferred_element_type=F32)
    acc[...] = jnp.zeros_like(acc)

    @functools.partial(loop, 0, BASE)
    def _(r):
        row = pl.multiple_of(r * NK, NK)
        value = jnp.concatenate([spread[part, pl.ds(row, NK), :] for part in range(3)], axis=0)
        high = value.astype(BF16).astype(F32)
        both = jnp.concatenate([high, value - high], axis=0).astype(BF16)
        acc[...] += over_lanes(both, tables[pl.ds(pl.multiple_of(r * PIX, PIX), PIX), :])

    back = acc[0:24, :] + acc[24:48, :]
    for k in range(NK):
        for part in range(3):
            for u in range(8):
                prow[8 * part + u : 8 * part + u + 1, :] = back[
                    NK * part + k : NK * part + k + 1, 128 * u : 128 * (u + 1)
                ]
        prow[24:32, :] = jnp.broadcast_to(share[k : k + 1, :], (8, 128))
        parts[k] = prow[...].astype(BF16)

    def sum_copy(g):
        return remote(parts.at[g], heap.at[c], sum_send.at[g], sum_recv.at[c], {"cls": 4 * g + home})

    def out_copy(d):
        target = lax.rem(j + d, PTCL)
        return remote(outbox.at[target], inbox.at[lane], out_send.at[d], out_recv.at[lane], row_peer(d))

    owners(lambda g: sum_copy(g).start())

    @pl.when(owner)
    def _():
        heap[c] = parts[mine]

        def arrive(d):
            source = lax.rem(c + d, CLS)
            remote(parts.at[0], heap.at[source], sum_send.at[0], sum_recv.at[source], {"cls": source}).wait_recv()

        loop(1, CLS, arrive)
        sums = lax.fori_loop(1, CLS, lambda i, t: t + heap[i].astype(F32), heap[0].astype(F32))
        below = sums[16:24] + 1.0
        planes = jnp.concatenate([sums[0:8] / below, sums[8:16] / below], axis=1)
        high = planes.astype(BF16).astype(F32)
        both = jnp.concatenate([high, planes - high], axis=0).astype(BF16)
        joined = jnp.dot(both, join_matrix(), preferred_element_type=F32)
        joined = joined[0:8] + joined[8:16]
        for b in range(PTCL):
            u, h = b // 2, b % 2
            outbox[b] = jnp.where(
                iota((8, 128), 0) == 0, joined[u : u + 1, 128 * h : 128 * (h + 1)], sums[24:25, :]
            )
        loop(1, PTCL, lambda d: out_copy(d).start())
        inbox[lane] = outbox[j]

    @functools.partial(loop, 0, 4)
    def _(i):
        @pl.when(first + i != j)
        def _():
            remote(outbox.at[0], inbox.at[i], out_send.at[0], out_recv.at[i], row_peer(1)).wait_recv()

    new_ref[...] = jnp.concatenate([inbox[i, 0:1, :] for i in range(4)], axis=0)
    share_row = inbox[0, 1:2, :]
    for i in range(1, 4):
        share_row = jnp.where(iota((1, 128), 1) == i, inbox[i, 1:2, :], share_row)
    share_ref[...] = share_row * (128.0 / 2048.0)

    loop(1, PTCL, lambda d: image_copy(d, j).wait_send())
    loop(1, PTCL, lambda d: stat_copy(d, j).wait_send())
    owners(lambda g: sum_copy(g).wait_send())

    @pl.when(owner)
    def _():
        loop(1, CLS, lambda d: ref_copy(d).wait_send())
        loop(1, PTCL, lambda d: out_copy(d).wait_send())


def on_device(images, references, log_prior, defocus, groups):
    vmem = pl.BlockSpec(memory_space=VMEM)
    dma = pltpu.SemaphoreType.DMA
    new, share = pl.pallas_call(
        em_kernel,
        out_shape=(jax.ShapeDtypeStruct((4, 128), F32), jax.ShapeDtypeStruct((1, 128), F32)),
        in_specs=[vmem] * 5,
        out_specs=(vmem, vmem),
        scratch_shapes=[
            VMEM((8, LANES), F32),
            VMEM((BASE * PIX, LANES), BF16),
            VMEM((4 * PIX, LANES), BF16),
            VMEM((NB, LANES), F32),
            VMEM((32, 128), F32),
            VMEM((32, 128), BF16),
            VMEM((PTCL, NB, 128), BF16),
            VMEM((NK, 32, 128), BF16),
            VMEM((NK * 32, 128), F32),
            VMEM((2 * NB, PIX), BF16),
            VMEM((2 * NK, PIX), BF16),
            VMEM((2, ROWS, LANES), F32),
            VMEM((3, 4 * NB, LANES), BF16),
            VMEM((4 * NB, LANES), BF16),
            VMEM((8, 128), F32),
            VMEM((PTCL, 8, 128), F32),
            VMEM((3, ROWS, LANES), F32),
            VMEM((48, PIX), F32),
            VMEM((32, 128), F32),
            VMEM((NK, 32, 128), BF16),
            VMEM((CLS, 32, 128), BF16),
            VMEM((PTCL, 8, 128), F32),
            VMEM((4, 8, 128), F32),
            dma((PTCL,)),
            dma((PTCL,)),
            dma((CLS,)),
            dma((NK,)),
            dma((PTCL,)),
            dma((PTCL,)),
            dma((NK,)),
            dma((CLS,)),
            dma((PTCL,)),
            dma((4,)),
        ],
        compiler_params=pltpu.CompilerParams(
            collective_id=0, has_side_effects=True, vmem_limit_bytes=60 << 20
        ),
        name="em",
    )(images, references, log_prior[None, :], defocus[None, :], groups[None, :])
    return new, share[0, :4]


def solution(mesh):
    return jax.shard_map(
        on_device,
        mesh=mesh,
        in_specs=(P("cls", "ptcl"), P("cls", None), P("cls"), P(), P("cls")),
        out_specs=(P("cls", "ptcl"), P("cls")),
        check_vma=False,
    )
```

time: 727 us -> 66.1 us (0.09)
  waiting for transfers between devices: 395 us -> 0 us
  blocking collectives: 196 us -> 0 us
  local copies, waits for them, and re-layouts: 92.5 us -> 1.71 us
  Pallas kernels: 0 us -> 63.6 us
  matrix products: 20.8 us -> 0 us
  between operations: 15.3 us -> 0.66 us
    unnamed x4 -> x0, waiting for transfers between devices: 228 us -> none
    unnamed x2 -> x0, blocking collectives: 123 us -> none
    reduce_scatter x1 -> x0, waiting for transfers between devices: 83.5 us -> none  [on_device(): owned = lax.psum_scatter(owned, 'ptcl', scatter_dimension=1, tiled=True)]
    psum x1 -> x0, waiting for transfers between devices: 83.1 us -> none  [on_device(): summed_scores = lax.psum(partial_scores, 'ptcl')]
    all_gather x1 -> x0, blocking collectives: 72.3 us -> none  [on_device(): lax.all_gather(references, 'cls', axis=0, tiled=True)]
    pallas_call x0 -> x1, Pallas kernels: none -> 63.6 us  [on_device(): pl.pallas_call(em_kernel, out_shape=(jax.ShapeDtypeStruct((4, 128), F32),...]
    reshape x7 -> x0, local copies, waits for them, and re-layouts: 44.1 us -> none  [the longest x2 31.2 us: on_device(): all_refs.reshape(class_count, pix_count, 2)]
    all_gather x1 -> x0, local copies, waits for them, and re-layouts: 27 us -> none  [on_device(): lax.all_gather(references, 'cls', axis=0, tiled=True)]
  transfers between devices with their start and end apart: 3 -> 0, of which waited for: 3 -> 0; matrix products, arithmetic and copies ran while one was open for 0% -> 0% of each run, Pallas kernels for 0% -> 0%
where the time goes in v2:
time: 66.1 us; the launch traced here: 65.9 us
  Pallas kernels  63.6 us (96%)
  local copies, waits for them, and re-layouts  1.71 us (3%)
    pallas_call x1, Pallas kernels, on_device(): pl.pallas_call(em_kernel, out_shape=(jax.ShapeDtypeStruct((4, 128), F32),...  63.6 us

profile of v2, /device:TPU:1, one launch (start us, length us, event | category | flops | bytes accessed | tf_op | source)
XLA Modules:
  0.0 65.9 jit_solution(15108009058255329063)
XLA Ops:
  0.6 63.6 %em.1 = (f32[4,128]{1,0:T(4,128)}, f32[1,128]{1,0:T(1,128)}) custom-call(bf16[64,128]{1,0:T(8,128)(2,1)} %img_ref.1, bf16[4,2048]{1,0:T(4,128)(2,1)} %ref_ref.1, bf16[1,4]{1,0:T(2,128)(2,1)} %bitcast.5, f32[1,32]{1,0:T(1,128)} %bitcast.6, s32[1,64]{1,0:T(1,128)} %bitcast.7), custom_call_target="tpu_custom_call" | custom-call | tf_op jit(solution)/shard_map/em/pallas_call | solution.py:364
  64.2 0.0 copy-start.1
  64.2 0.0 copy-start
  64.2 0.6 copy-done.1
  64.8 0.5 slice_bitcast_fusion
  65.4 0.0 copy-done
  65.4 0.6 copy.8
Async XLA Ops:
  64.2 0.6 copy-start.1
  64.2 1.1 %copy-start = (f32[4,128]{1,0:T(4,128)S(1)}, f32[4,128]{1,0:T(4,128)}, u32[]{:S(2)}) copy-start(f32[4,128]{1,0:T(4,128)} %get-tuple-element.8) | copy-start | bytes 6148

commit v3 on v2

--- a/solution.py
+++ b/solution.py
@@ -14,8 +14,9 @@
 ROT = 36
 BASE = ROT // 4
 EXT = SIDE + 1
-LANES = 1152
-CHUNK = 384
+PATCH = 11
+PATCHES = 9
+LANES = 128 * PATCHES
 CLS = 32
 PTCL = 16
 NK = 8
@@ -31,11 +32,24 @@
 SINES = [float(x) for x in np.sin(ANGLES).astype(np.float32)]
 
 
-def choose(values, r):
-    out = jnp.float32(values[0])
-    for i, value in enumerate(values[1:], 1):
-        out = jnp.where(r == i, jnp.float32(value), out)
-    return out
+def bands():
+    out, offset = [], 0
+    for r in range(BASE):
+        for patch in range(PATCHES):
+            down = np.arange(PATCH)[:, None] + PATCH * (patch // 3) - SIDE // 2
+            across = np.arange(PATCH)[None, :] + PATCH * (patch % 3) - SIDE // 2
+            source = COSINES[r] * down - SINES[r] * across
+            low = max(int(np.floor(source.min() - 1e-3)) + SIDE // 2, 0)
+            high = min(int(np.floor(source.max() + 1e-3)) + 1 + SIDE // 2, SIDE - 1)
+            count = high // 4 - low // 4 + 1
+            out.append((r, patch, low // 4, count, offset))
+            offset += count
+    return out, offset
+
+
+BANDS, BLOCKS = bands()
+TOUCH = [[(r, patch) for r, patch, g, n, _ in BANDS if g <= group < g + n] for group in range(8)]
+STARTS = [sum(len(t) for t in TOUCH[:group]) for group in range(9)]
 
 
 def iota(shape, axis):
@@ -43,16 +57,19 @@
 
 
 def grid_rows(grid):
-    e = iota((1, LANES), 1).astype(F32)
-    down = jnp.floor((e + 0.5) * (1.0 / EXT))
-    across = e - EXT * down - SIDE // 2
-    down = down - SIDE // 2
+    column = iota((1, LANES), 1)
+    patch = (column // 128).astype(F32)
+    inner = (column % 128).astype(F32)
+    patch_down = jnp.floor((patch + 0.5) * (1.0 / 3.0))
+    inner_down = jnp.floor((inner + 0.5) * (1.0 / PATCH))
+    down = PATCH * patch_down + inner_down - SIDE // 2
+    across = PATCH * (patch - 3.0 * patch_down) + inner - PATCH * inner_down - SIDE // 2
     grid[0:1, :] = across
     grid[1:2, :] = down
     grid[2:3, :] = (across * across + down * down) * (1.0 / (SIDE // 2) ** 2)
     a, d = across, down
     for s in range(4):
-        inside = (a >= -16.0) & (a <= 15.0) & (d >= -16.0) & (d <= 15.0)
+        inside = (a >= -16.0) & (a <= 15.0) & (d >= -16.0) & (d <= 15.0) & (inner < PATCH * PATCH - 0.5)
         grid[4 + s : 5 + s, :] = jnp.where(inside, (d + 16.0) * SIDE + a + 16.0, -1.0)
         a, d = -d, a
 
@@ -84,21 +101,23 @@
 
 
 def make_tables(grid, tables):
-    def step(i, _):
-        r = i // (LANES // CHUNK)
-        start = pl.multiple_of((i % (LANES // CHUNK)) * CHUNK, CHUNK)
-        cosine, sine = choose(COSINES, r), choose(SINES, r)
-        qa = grid[0:1, pl.ds(start, CHUNK)]
-        qd = grid[1:2, pl.ds(start, CHUNK)]
-        place = iota((SIDE, CHUNK), 0).astype(F32) - float(SIDE // 2)
-        hat_a = jnp.maximum(0.0, 1.0 - jnp.abs(cosine * qa + sine * qd - place))
-        hat_d = jnp.maximum(0.0, 1.0 - jnp.abs(cosine * qd - sine * qa - place))
-        row = pl.multiple_of(r * PIX, PIX)
-        for p in range(SIDE):
-            tables[pl.ds(row + p * SIDE, SIDE), pl.ds(start, CHUNK)] = (hat_a * hat_d[p : p + 1, :]).astype(BF16)
-        return 0
-
-    lax.fori_loop(0, BASE * (LANES // CHUNK), step, 0)
+    place = iota((SIDE, 128), 0).astype(F32) - float(SIDE // 2)
+    for r, patch, group, count, offset in BANDS:
+        qa = grid[0:1, 128 * patch : 128 * (patch + 1)]
+        qd = grid[1:2, 128 * patch : 128 * (patch + 1)]
+        hat_a = jnp.maximum(0.0, 1.0 - jnp.abs(COSINES[r] * qa + SINES[r] * qd - place))
+        line = iota((8 * ((count + 1) // 2), 128), 0).astype(F32) + float(4 * group - SIDE // 2)
+        hat_d = jnp.maximum(0.0, 1.0 - jnp.abs(COSINES[r] * qd - SINES[r] * qa - line))
+        for p in range(4 * count):
+            row = 128 * offset + SIDE * p
+            tables[row : row + SIDE, :] = (hat_a * hat_d[p : p + 1, :]).astype(BF16)
+
+
+def turn_tables(tables, tables_t):
+    for r, patch, group, count, offset in BANDS:
+        for i in range(count):
+            place = STARTS[group + i] + TOUCH[group + i].index((r, patch))
+            tables_t[128 * place : 128 * (place + 1), :] = tables[128 * (offset + i) : 128 * (offset + i + 1), :].T
 
 
 def make_picks(grid, picks):
@@ -114,8 +133,8 @@
 def em_kernel(
     img_ref, ref_ref, prior_ref, focus_ref, group_ref,
     new_ref, share_ref,
-    grid, tables, picks, contrast, mrow, message, imgs, refs, flat, wide, refmat, turned, vals, square_lo,
-    stat, stats, spread, acc, prow, parts, heap, outbox, inbox,
+    grid, tables, tables_t, picks, contrast, mrow, message, imgs, refs, flat, wide, refmat, turned, vals, square_lo,
+    stat, stats, spread, rows, parts, heap, outbox, inbox,
     img_send, img_recv, ref_send, ref_recv, stat_send, stat_recv, sum_send, sum_recv, out_send, out_recv,
 ):
     c = lax.axis_index("cls")
@@ -133,9 +152,14 @@
 
         lax.fori_loop(low, high, step, 0)
 
+    def farthest(count, body):
+        loop(0, count - 1, lambda i: body(count // 2 + ((i + 1) // 2) * (2 * (i % 2) - 1)))
+
     def owners(body):
         @functools.partial(loop, 0, NK)
-        def _(g):
+        def _(i):
+            g = lax.rem(mine + NK // 2 + ((i + 1) // 2) * (2 * (i % 2) - 1) + NK, NK)
+
             @pl.when(4 * g + home != c)
             def _():
                 body(g)
@@ -155,14 +179,14 @@
 
     @pl.when(owner)
     def _():
-        loop(1, CLS, lambda d: pl.semaphore_signal(barrier, inc=1, device_id=column_peer(d), device_id_type=MESH))
+        farthest(CLS, lambda d: pl.semaphore_signal(barrier, inc=1, device_id=column_peer(d), device_id_type=MESH))
 
     @pl.when(jnp.logical_not(owner))
     def _():
-        loop(0, NK, lambda g: pl.semaphore_signal(
+        owners(lambda g: pl.semaphore_signal(
             barrier, inc=1, device_id={"cls": 4 * g + home}, device_id_type=MESH))
 
-    loop(1, PTCL, lambda d: pl.semaphore_signal(barrier, inc=1, device_id=row_peer(d), device_id_type=MESH))
+    farthest(PTCL, lambda d: pl.semaphore_signal(barrier, inc=1, device_id=row_peer(d), device_id_type=MESH))
 
     split = split_matrix()
     chosen = jnp.sum(
@@ -200,11 +224,12 @@
 
     @pl.when(owner)
     def _():
-        loop(1, CLS, lambda d: ref_copy(d).start())
+        farthest(CLS, lambda d: ref_copy(d).start())
         refs[mine] = message[...]
 
-    loop(1, PTCL, lambda d: image_copy(d, j).start())
+    farthest(PTCL, lambda d: image_copy(d, j).start())
     imgs[j] = img_ref[...]
+    turn_tables(tables, tables_t)
     loop(1, PTCL, lambda d: image_copy(d, lax.rem(j + PTCL - d, PTCL)).wait_recv())
 
     for u in range(8):
@@ -236,15 +261,15 @@
         refmat[:, 128 * u : 128 * (u + 1)] = jnp.concatenate([real, imag], axis=0).astype(BF16)
     prior = flat[pl.ds(16, NK, stride=32), :]
 
-    @functools.partial(loop, 0, BASE)
-    def _(r):
+    for r, patch, group, count, offset in BANDS:
         both = jnp.dot(
-            refmat[...], tables[pl.ds(pl.multiple_of(r * PIX, PIX), PIX), :], preferred_element_type=F32
+            refmat[:, 128 * group : 128 * (group + count)],
+            tables[128 * offset : 128 * (offset + count), :],
+            preferred_element_type=F32,
         )
         both = both.astype(BF16).astype(F32)
-        row = pl.multiple_of(r * NK, NK)
-        turned[0, pl.ds(row, NK), :] = both[:NK]
-        turned[1, pl.ds(row, NK), :] = both[NK:]
+        turned[0, NK * r : NK * (r + 1), 128 * patch : 128 * (patch + 1)] = both[:NK]
+        turned[1, NK * r : NK * (r + 1), 128 * patch : 128 * (patch + 1)] = both[NK:]
 
     real, imag = turned[0], turned[1]
     match = over_lanes(real.astype(BF16), vals[0]) + over_lanes(imag.astype(BF16), vals[1])
@@ -267,7 +292,7 @@
     def stat_copy(d, slot):
         return remote(stat, stats.at[slot], stat_send.at[d], stat_recv.at[d], row_peer(d))
 
-    loop(1, PTCL, lambda d: stat_copy(d, j).start())
+    farthest(PTCL, lambda d: stat_copy(d, j).start())
     stats[j] = stat[...]
     loop(1, PTCL, lambda d: stat_copy(d, lax.rem(j + PTCL - d, PTCL)).wait_recv())
     peaks = stats[:, 0:1, :]
@@ -283,25 +308,25 @@
 
     for part in range(3):
         spread[part] = jnp.dot(weights, vals[part], preferred_element_type=F32)
-    acc[...] = jnp.zeros_like(acc)
-
-    @functools.partial(loop, 0, BASE)
-    def _(r):
-        row = pl.multiple_of(r * NK, NK)
-        value = jnp.concatenate([spread[part, pl.ds(row, NK), :] for part in range(3)], axis=0)
+    split_sums = []
+    for r in range(BASE):
+        value = jnp.concatenate([spread[part, NK * r : NK * (r + 1), :] for part in range(3)], axis=0)
         high = value.astype(BF16).astype(F32)
-        both = jnp.concatenate([high, value - high], axis=0).astype(BF16)
-        acc[...] += over_lanes(both, tables[pl.ds(pl.multiple_of(r * PIX, PIX), PIX), :])
-
-    back = acc[0:24, :] + acc[24:48, :]
+        split_sums.append(jnp.concatenate([high, value - high], axis=0).astype(BF16))
+    for group in range(8):
+        points = jnp.concatenate(
+            [split_sums[r][:, 128 * patch : 128 * (patch + 1)] for r, patch in TOUCH[group]], axis=1
+        )
+        back = jnp.dot(
+            points, tables_t[128 * STARTS[group] : 128 * STARTS[group + 1], :], preferred_element_type=F32
+        )
+        back = back[0:24] + back[24:48]
+        for part in range(3):
+            rows[pl.ds(8 * part + group, NK, stride=32), :] = back[NK * part : NK * (part + 1), :]
+    for i in range(24, 32):
+        rows[pl.ds(i, NK, stride=32), :] = jnp.broadcast_to(share, (NK, 128))
     for k in range(NK):
-        for part in range(3):
-            for u in range(8):
-                prow[8 * part + u : 8 * part + u + 1, :] = back[
-                    NK * part + k : NK * part + k + 1, 128 * u : 128 * (u + 1)
-                ]
-        prow[24:32, :] = jnp.broadcast_to(share[k : k + 1, :], (8, 128))
-        parts[k] = prow[...].astype(BF16)
+        parts[k] = rows[32 * k : 32 * (k + 1), :].astype(BF16)
 
     def sum_copy(g):
         return remote(parts.at[g], heap.at[c], sum_send.at[g], sum_recv.at[c], {"cls": 4 * g + home})
@@ -333,7 +358,7 @@
             outbox[b] = jnp.where(
                 iota((8, 128), 0) == 0, joined[u : u + 1, 128 * h : 128 * (h + 1)], sums[24:25, :]
             )
-        loop(1, PTCL, lambda d: out_copy(d).start())
+        farthest(PTCL, lambda d: out_copy(d).start())
         inbox[lane] = outbox[j]
 
     @functools.partial(loop, 0, 4)
@@ -368,7 +393,8 @@
         out_specs=(vmem, vmem),
         scratch_shapes=[
             VMEM((8, LANES), F32),
-            VMEM((BASE * PIX, LANES), BF16),
+            VMEM((BLOCKS * 128, 128), BF16),
+            VMEM((BLOCKS * 128, 128), BF16),
             VMEM((4 * PIX, LANES), BF16),
             VMEM((NB, LANES), F32),
             VMEM((32, 128), F32),
@@ -384,8 +410,7 @@
             VMEM((8, 128), F32),
             VMEM((PTCL, 8, 128), F32),
             VMEM((3, ROWS, LANES), F32),
-            VMEM((48, PIX), F32),
-            VMEM((32, 128), F32),
+            VMEM((NK * 32, 128), F32),
             VMEM((NK, 32, 128), BF16),
             VMEM((CLS, 32, 128), BF16),
             VMEM((PTCL, 8, 128), F32),

time: 66.1 us -> 56.9 us (0.86)
  Pallas kernels: 63.6 us -> 54.3 us
    pallas_call x1, Pallas kernels: 63.6 us -> 54.3 us  [on_device(): pl.pallas_call(em_kernel, out_shape=(jax.ShapeDtypeStruct((4, 128), F32),...]
where the time goes in v3:
time: 56.9 us; the launch traced here: 56.7 us
  Pallas kernels  54.3 us (95%)
  local copies, waits for them, and re-layouts  1.71 us (3%)
  between operations  0.66 us (1%)
    pallas_call x1, Pallas kernels, on_device(): pl.pallas_call(em_kernel, out_shape=(jax.ShapeDtypeStruct((4, 128), F32),...  54.3 us
    unnamed x5, local copies, waits for them, and re-layouts  1.2 us

profile of v3, /device:TPU:1, one launch (start us, length us, event | category | flops | bytes accessed | tf_op | source)
XLA Modules:
  0.0 56.7 jit_solution(12592729566421457415)
XLA Ops:
  0.6 54.3 %em.1 = (f32[4,128]{1,0:T(4,128)}, f32[1,128]{1,0:T(1,128)}) custom-call(bf16[64,128]{1,0:T(8,128)(2,1)} %img_ref.1, bf16[4,2048]{1,0:T(4,128)(2,1)} %ref_ref.1, bf16[1,4]{1,0:T(2,128)(2,1)} %bitcast.5, f32[1,32]{1,0:T(1,128)} %bitcast.6, s32[1,64]{1,0:T(1,128)} %bitcast.7), custom_call_target="tpu_custom_call" | custom-call | tf_op jit(solution)/shard_map/em/pallas_call | solution.py:389
  55.0 0.0 copy-start.1
  55.0 0.0 copy-start
  55.0 0.6 %copy-done.1 = f32[1,128]{1,0:T(1,128)S(1)} copy-done((f32[1,128]{1,0:T(1,128)S(1)}, f32[1,128]{1,0:T(1,128)}, u32[]{:S(2)}) %copy-start.1) | copy-done | bytes 536
  55.6 0.5 slice_bitcast_fusion
  56.1 0.0 copy-done
  56.1 0.6 %copy.8 = f32[4,128]{1,0:T(4,128)} copy(f32[4,128]{1,0:T(4,128)S(1)} %copy-done) | data formatting | bytes 4096
Async XLA Ops:
  55.0 0.6 %copy-start.1 = (f32[1,128]{1,0:T(1,128)S(1)}, f32[1,128]{1,0:T(1,128)}, u32[]{:S(2)}) copy-start(f32[1,128]{1,0:T(1,128)} %get-tuple-element.5) | copy-start | bytes 1540
  55.0 1.1 %copy-start = (f32[4,128]{1,0:T(4,128)S(1)}, f32[4,128]{1,0:T(4,128)}, u32[]{:S(2)}) copy-start(f32[4,128]{1,0:T(4,128)} %get-tuple-element.8) | copy-start | bytes 6148

commit v4 on v3

--- a/solution.py
+++ b/solution.py
@@ -20,6 +20,7 @@
 CLS = 32
 PTCL = 16
 NK = 8
+NEAR = 17
 ROWS = BASE * NK
 NB = 64
 MESH = pl.DeviceIdType.MESH
@@ -131,10 +132,11 @@
 
 
 def em_kernel(
-    img_ref, ref_ref, prior_ref, focus_ref, group_ref,
+    img_in, ref_in, prior_in, focus_in, group_in,
     new_ref, share_ref,
     grid, tables, tables_t, picks, contrast, mrow, message, imgs, refs, flat, wide, refmat, turned, vals, square_lo,
     stat, stats, spread, rows, parts, heap, outbox, inbox,
+    img_ref, ref_ref, prior_ref, focus_ref, group_ref, fetched,
     img_send, img_recv, ref_send, ref_recv, stat_send, stat_recv, sum_send, sum_recv, out_send, out_recv,
 ):
     c = lax.axis_index("cls")
@@ -175,18 +177,27 @@
             src_ref=src, dst_ref=dst, send_sem=send, recv_sem=recv, device_id=device, device_id_type=MESH
         )
 
+    fetches = [
+        pltpu.make_async_copy(source, place, fetched.at[i])
+        for i, (source, place) in enumerate(
+            [(ref_in, ref_ref), (prior_in, prior_ref), (img_in, img_ref), (focus_in, focus_ref), (group_in, group_ref)]
+        )
+    ]
+    for fetch in fetches:
+        fetch.start()
+
     barrier = pltpu.get_barrier_semaphore()
-
-    @pl.when(owner)
-    def _():
-        farthest(CLS, lambda d: pl.semaphore_signal(barrier, inc=1, device_id=column_peer(d), device_id_type=MESH))
-
-    @pl.when(jnp.logical_not(owner))
-    def _():
-        owners(lambda g: pl.semaphore_signal(
-            barrier, inc=1, device_id={"cls": 4 * g + home}, device_id_type=MESH))
+    z, x = c // 2, lax.rem(c, 2)
+
+    @functools.partial(owners)
+    def _(g):
+        @pl.when(lax.rem(2 * g + home // 2 - z + 20, 16) <= 8)
+        def _():
+            pl.semaphore_signal(barrier, inc=1, device_id={"cls": 4 * g + home}, device_id_type=MESH)
 
     farthest(PTCL, lambda d: pl.semaphore_signal(barrier, inc=1, device_id=row_peer(d), device_id_type=MESH))
+    for fetch in fetches:
+        fetch.wait()
 
     split = split_matrix()
     chosen = jnp.sum(
@@ -198,6 +209,43 @@
     mrow[16:32, :] = jnp.broadcast_to(own_prior, (16, 128))
     message[...] = mrow[...].astype(BF16)
     grid_rows(grid)
+    @pl.when(owner)
+    def _():
+        pl.semaphore_wait(barrier, PTCL - 1 + NEAR)
+
+    @pl.when(jnp.logical_not(owner))
+    def _():
+        pl.semaphore_wait(barrier, PTCL - 1)
+
+    def near(dz, flip):
+        return {"cls": 2 * lax.rem(z + dz + 16, 16) + lax.rem(x + flip, 2)}
+
+    def ref_copy(i):
+        target = near((4 - i // 4) * (1 - 2 * ((i // 2) % 2)), lax.rem(i + 1, 2))
+        return remote(message, refs.at[mine], ref_send.at[i], ref_recv.at[mine], target)
+
+    behind, ahead = lax.rem(mine + NK - 2, NK), lax.rem(mine + 2, NK)
+
+    def pass_on(i):
+        source = jnp.where(i < 8, behind, ahead)
+        target = near(jnp.where(i < 8, 4 - i // 2, i // 2 - 7), lax.rem(i, 2))
+        return remote(refs.at[source], refs.at[source], ref_send.at[NEAR + i], ref_recv.at[source], target)
+
+    def ref_arrives(g):
+        remote(message, refs.at[g], ref_send.at[0], ref_recv.at[g], column_peer(1)).wait_recv()
+
+    def image_copy(d, slot):
+        return remote(img_ref, imgs.at[slot], img_send.at[d], img_recv.at[d], row_peer(d))
+
+    @pl.when(owner)
+    def _():
+        loop(0, NEAR, lambda i: ref_copy(i).start())
+        refs[mine] = message[...]
+
+    farthest(PTCL, lambda d: image_copy(d, j).start())
+    imgs[j] = img_ref[...]
+
+    make_tables(grid, tables)
     group = column_of(group_ref[...].astype(F32), NB)
     groups_count = focus_ref.shape[1]
     focus = jnp.sum(
@@ -205,31 +253,15 @@
     )
     phase = math.pi * focus * grid[2:3, :]
     contrast[...] = -(0.99499 * jnp.sin(phase) + 0.1 * jnp.cos(phase))
-    make_tables(grid, tables)
     make_picks(grid, picks)
 
     @pl.when(owner)
     def _():
-        pl.semaphore_wait(barrier, PTCL - 1 + CLS - 1)
-
-    @pl.when(jnp.logical_not(owner))
-    def _():
-        pl.semaphore_wait(barrier, PTCL - 1 + NK)
-
-    def ref_copy(d):
-        return remote(message, refs.at[mine], ref_send.at[d], ref_recv.at[mine], column_peer(d))
-
-    def image_copy(d, slot):
-        return remote(img_ref, imgs.at[slot], img_send.at[d], img_recv.at[d], row_peer(d))
-
-    @pl.when(owner)
-    def _():
-        farthest(CLS, lambda d: ref_copy(d).start())
-        refs[mine] = message[...]
-
-    farthest(PTCL, lambda d: image_copy(d, j).start())
-    imgs[j] = img_ref[...]
-    turn_tables(tables, tables_t)
+        ref_arrives(behind)
+        loop(0, 8, lambda i: pass_on(i).start())
+        ref_arrives(ahead)
+        loop(8, 14, lambda i: pass_on(i).start())
+
     loop(1, PTCL, lambda d: image_copy(d, lax.rem(j + PTCL - d, PTCL)).wait_recv())
 
     for u in range(8):
@@ -251,7 +283,12 @@
         vals[2, pl.ds(row, NB), :] = high
         square_lo[pl.ds(row, NB), :] = (square - high.astype(F32)).astype(BF16)
 
-    owners(lambda g: remote(message, refs.at[g], ref_send.at[0], ref_recv.at[g], column_peer(1)).wait_recv())
+    @functools.partial(owners)
+    def _(g):
+        @pl.when(jnp.logical_not(owner) | ((g != behind) & (g != ahead)))
+        def _():
+            ref_arrives(g)
+
 
     flat[...] = jnp.dot(refs[...].reshape(NK * 32, 128), split, preferred_element_type=F32)
     for u in range(8):
@@ -294,6 +331,7 @@
 
     farthest(PTCL, lambda d: stat_copy(d, j).start())
     stats[j] = stat[...]
+    turn_tables(tables, tables_t)
     loop(1, PTCL, lambda d: stat_copy(d, lax.rem(j + PTCL - d, PTCL)).wait_recv())
     peaks = stats[:, 0:1, :]
     peak = jnp.max(peaks, axis=0)
@@ -379,7 +417,8 @@
 
     @pl.when(owner)
     def _():
-        loop(1, CLS, lambda d: ref_copy(d).wait_send())
+        loop(0, NEAR, lambda i: ref_copy(i).wait_send())
+        loop(0, 14, lambda i: pass_on(i).wait_send())
         loop(1, PTCL, lambda d: out_copy(d).wait_send())
 
 
@@ -388,8 +427,8 @@
     dma = pltpu.SemaphoreType.DMA
     new, share = pl.pallas_call(
         em_kernel,
-        out_shape=(jax.ShapeDtypeStruct((4, 128), F32), jax.ShapeDtypeStruct((1, 128), F32)),
-        in_specs=[vmem] * 5,
+        out_shape=(VMEM((4, 128), F32), VMEM((1, 128), F32)),
+        in_specs=[pl.BlockSpec(memory_space=pl.ANY)] * 5,
         out_specs=(vmem, vmem),
         scratch_shapes=[
             VMEM((8, LANES), F32),
@@ -415,6 +454,12 @@
             VMEM((CLS, 32, 128), BF16),
             VMEM((PTCL, 8, 128), F32),
             VMEM((4, 8, 128), F32),
+            VMEM((NB, 128), BF16),
+            VMEM((4, 2 * PIX), BF16),
+            VMEM((1, 4), BF16),
+            VMEM((1, defocus.shape[0]), F32),
+            VMEM((1, NB), jnp.int32),
+            dma((5,)),
             dma((PTCL,)),
             dma((PTCL,)),
             dma((CLS,)),

time: 56.9 us -> 52.1 us (0.916)
  Pallas kernels: 54.3 us -> 50.1 us
  local copies, waits for them, and re-layouts: 1.71 us -> 1.09 us
    pallas_call x1, Pallas kernels: 54.3 us -> 50.1 us  [on_device(): pl.pallas_call(em_kernel, out_shape=(VMEM((4, 128), F32), VMEM((1, 128),...]
    unnamed x5 -> x1, local copies, waits for them, and re-layouts: 1.2 us -> 0.58 us
where the time goes in v4:
time: 52.1 us; the launch traced here: 51.9 us
  Pallas kernels  50.1 us (96%)
  local copies, waits for them, and re-layouts  1.09 us (2%)
  between operations  0.64 us (1%)
    pallas_call x1, Pallas kernels, on_device(): pl.pallas_call(em_kernel, out_shape=(VMEM((4, 128), F32), VMEM((1, 128),...  50.1 us

profile of v4, /device:TPU:1, one launch (start us, length us, event | category | flops | bytes accessed | tf_op | source)
XLA Modules:
  0.0 51.9 jit_solution(8378353338570618629)
XLA Ops:
  0.6 50.1 %em.1 = (f32[4,128]{1,0:T(4,128)S(1)}, f32[1,128]{1,0:T(1,128)S(1)}) custom-call(bf16[64,128]{1,0:T(8,128)(2,1)} %img_in.1, bf16[4,2048]{1,0:T(4,128)(2,1)} %ref_in.1, bf16[1,4]{1,0:T(2,128)(2,1)} %bitcast.5, f32[1,32]{1,0:T(1,128)} %bitcast.6, s32[1,64]{1,0:T(1,128)} %bitcast.7), custom_call_target="tpu_custom_call" | custom-call | tf_op jit(solution)/shard_map/em/pallas_call | solution.py:428
  50.8 0.6 %copy.8 = f32[4,128]{1,0:T(4,128)} copy(f32[4,128]{1,0:T(4,128)S(1)} %get-tuple-element.6) | data formatting | bytes 4096
  51.4 0.5 slice_bitcast_fusion

commit v5 on v4

--- a/solution.py
+++ b/solution.py
@@ -191,7 +191,9 @@
 
     @functools.partial(owners)
     def _(g):
-        @pl.when(lax.rem(2 * g + home // 2 - z + 20, 16) <= 8)
+        other = 2 * g + home // 2
+
+        @pl.when((lax.rem(other - z + 20, 16) <= 8) | (other > z))
         def _():
             pl.semaphore_signal(barrier, inc=1, device_id={"cls": 4 * g + home}, device_id_type=MESH)
 
@@ -209,14 +211,6 @@
     mrow[16:32, :] = jnp.broadcast_to(own_prior, (16, 128))
     message[...] = mrow[...].astype(BF16)
     grid_rows(grid)
-    @pl.when(owner)
-    def _():
-        pl.semaphore_wait(barrier, PTCL - 1 + NEAR)
-
-    @pl.when(jnp.logical_not(owner))
-    def _():
-        pl.semaphore_wait(barrier, PTCL - 1)
-
     def near(dz, flip):
         return {"cls": 2 * lax.rem(z + dz + 16, 16) + lax.rem(x + flip, 2)}
 
@@ -231,36 +225,80 @@
         target = near(jnp.where(i < 8, 4 - i // 2, i // 2 - 7), lax.rem(i, 2))
         return remote(refs.at[source], refs.at[source], ref_send.at[NEAR + i], ref_recv.at[source], target)
 
+    def passed(low, high, body):
+        @functools.partial(loop, low, high)
+        def _(i):
+            start = jnp.where(i < 8, lax.rem(z + 12, 16), lax.rem(z + 4, 16))
+
+            @pl.when(start + jnp.where(i < 8, 8 - i // 2, 5 + i // 2) < 16)
+            def _():
+                body(pass_on(i))
+
+    def far_copies(body):
+        @functools.partial(loop, 0, 14)
+        def _(i):
+            k = 5 + i // 2
+
+            @pl.when(z + k >= 16)
+            def _():
+                body(remote(
+                    message, refs.at[mine], ref_send.at[NEAR + 14 + i], ref_recv.at[mine], near(k, lax.rem(i, 2))
+                ))
+
     def ref_arrives(g):
         remote(message, refs.at[g], ref_send.at[0], ref_recv.at[g], column_peer(1)).wait_recv()
 
     def image_copy(d, slot):
         return remote(img_ref, imgs.at[slot], img_send.at[d], img_recv.at[d], row_peer(d))
 
-    @pl.when(owner)
-    def _():
-        loop(0, NEAR, lambda i: ref_copy(i).start())
-        refs[mine] = message[...]
-
-    farthest(PTCL, lambda d: image_copy(d, j).start())
-    imgs[j] = img_ref[...]
-
-    make_tables(grid, tables)
-    group = column_of(group_ref[...].astype(F32), NB)
-    groups_count = focus_ref.shape[1]
-    focus = jnp.sum(
-        jnp.where(group == iota((NB, groups_count), 1).astype(F32), focus_ref[...], 0.0), axis=1, keepdims=True
-    )
-    phase = math.pi * focus * grid[2:3, :]
-    contrast[...] = -(0.99499 * jnp.sin(phase) + 0.1 * jnp.cos(phase))
-    make_picks(grid, picks)
-
-    @pl.when(owner)
-    def _():
-        ref_arrives(behind)
-        loop(0, 8, lambda i: pass_on(i).start())
-        ref_arrives(ahead)
-        loop(8, 14, lambda i: pass_on(i).start())
+    def prepare():
+        make_tables(grid, tables)
+        group = column_of(group_ref[...].astype(F32), NB)
+        groups_count = focus_ref.shape[1]
+        focus = jnp.sum(
+            jnp.where(group == iota((NB, groups_count), 1).astype(F32), focus_ref[...], 0.0), axis=1, keepdims=True
+        )
+        phase = math.pi * focus * grid[2:3, :]
+        contrast[...] = -(0.99499 * jnp.sin(phase) + 0.1 * jnp.cos(phase))
+        make_picks(grid, picks)
+
+    def send_out():
+        @pl.when(owner)
+        def _():
+            pl.semaphore_wait(barrier, PTCL - 1 + NEAR + 2 * jnp.clip(z - 4, 0, 7))
+            far_copies(lambda copy: copy.start())
+            loop(0, NEAR, lambda i: ref_copy(i).start())
+
+        @pl.when(jnp.logical_not(owner))
+        def _():
+            pl.semaphore_wait(barrier, PTCL - 1)
+
+        farthest(PTCL, lambda d: image_copy(d, j).start())
+
+        @pl.when(owner)
+        def _():
+            refs[mine] = message[...]
+
+        imgs[j] = img_ref[...]
+
+        @pl.when(owner)
+        def _():
+            ref_arrives(behind)
+            passed(0, 8, lambda copy: copy.start())
+            ref_arrives(ahead)
+            passed(8, 14, lambda copy: copy.start())
+
+    last = ((z >= 7) & (z <= 11)).astype(jnp.int32)
+
+    @functools.partial(loop, 0, 2)
+    def _(turn):
+        @pl.when(turn == last)
+        def _():
+            prepare()
+
+        @pl.when(turn == 0)
+        def _():
+            send_out()
 
     loop(1, PTCL, lambda d: image_copy(d, lax.rem(j + PTCL - d, PTCL)).wait_recv())
 
@@ -332,6 +370,14 @@
     farthest(PTCL, lambda d: stat_copy(d, j).start())
     stats[j] = stat[...]
     turn_tables(tables, tables_t)
+    loop(1, PTCL, lambda d: image_copy(d, j).wait_send())
+
+    @pl.when(owner)
+    def _():
+        loop(0, NEAR, lambda i: ref_copy(i).wait_send())
+        passed(0, 14, lambda copy: copy.wait_send())
+        far_copies(lambda copy: copy.wait_send())
+
     loop(1, PTCL, lambda d: stat_copy(d, lax.rem(j + PTCL - d, PTCL)).wait_recv())
     peaks = stats[:, 0:1, :]
     peak = jnp.max(peaks, axis=0)
@@ -374,17 +420,16 @@
         return remote(outbox.at[target], inbox.at[lane], out_send.at[d], out_recv.at[lane], row_peer(d))
 
     owners(lambda g: sum_copy(g).start())
+    loop(1, PTCL, lambda d: stat_copy(d, j).wait_send())
 
     @pl.when(owner)
     def _():
-        heap[c] = parts[mine]
-
-        def arrive(d):
-            source = lax.rem(c + d, CLS)
+        def arrive(i, total):
+            source = lax.rem(c + CLS + ((i + 2) // 2) * (1 - 2 * lax.rem(i, 2)), CLS)
             remote(parts.at[0], heap.at[source], sum_send.at[0], sum_recv.at[source], {"cls": source}).wait_recv()
-
-        loop(1, CLS, arrive)
-        sums = lax.fori_loop(1, CLS, lambda i, t: t + heap[i].astype(F32), heap[0].astype(F32))
+            return total + heap[source].astype(F32)
+
+        sums = lax.fori_loop(0, CLS - 1, arrive, parts[mine].astype(F32))
         below = sums[16:24] + 1.0
         planes = jnp.concatenate([sums[0:8] / below, sums[8:16] / below], axis=1)
         high = planes.astype(BF16).astype(F32)
@@ -399,6 +444,8 @@
         farthest(PTCL, lambda d: out_copy(d).start())
         inbox[lane] = outbox[j]
 
+    owners(lambda g: sum_copy(g).wait_send())
+
     @functools.partial(loop, 0, 4)
     def _(i):
         @pl.when(first + i != j)
@@ -411,14 +458,9 @@
         share_row = jnp.where(iota((1, 128), 1) == i, inbox[i, 1:2, :], share_row)
     share_ref[...] = share_row * (128.0 / 2048.0)
 
-    loop(1, PTCL, lambda d: image_copy(d, j).wait_send())
-    loop(1, PTCL, lambda d: stat_copy(d, j).wait_send())
-    owners(lambda g: sum_copy(g).wait_send())
 
     @pl.when(owner)
     def _():
-        loop(0, NEAR, lambda i: ref_copy(i).wait_send())
-        loop(0, 14, lambda i: pass_on(i).wait_send())
         loop(1, PTCL, lambda d: out_copy(d).wait_send())
 
 
@@ -462,7 +504,7 @@
             dma((5,)),
             dma((PTCL,)),
             dma((PTCL,)),
-            dma((CLS,)),
+            dma((NEAR + 28,)),
             dma((NK,)),
             dma((PTCL,)),
             dma((PTCL,)),

time: 52.1 us -> 56.4 us (1.083)
  Pallas kernels: 50.1 us -> 54.5 us
    pallas_call x1, Pallas kernels: 50.1 us -> 54.5 us  [on_device(): pl.pallas_call(em_kernel, out_shape=(VMEM((4, 128), F32), VMEM((1, 128),...]
where the time goes in v5:
time: 56.4 us; the launch traced here: 56.2 us
  Pallas kernels  54.5 us (97%)
  local copies, waits for them, and re-layouts  1.09 us (2%)
  between operations  0.64 us (1%)
    pallas_call x1, Pallas kernels, on_device(): pl.pallas_call(em_kernel, out_shape=(VMEM((4, 128), F32), VMEM((1, 128),...  54.5 us

profile of v5, /device:TPU:1, one launch (start us, length us, event | category | flops | bytes accessed | tf_op | source)
XLA Modules:
  0.0 56.2 jit_solution(16469421091067011714)
XLA Ops:
  0.6 54.5 %em.1 = (f32[4,128]{1,0:T(4,128)S(1)}, f32[1,128]{1,0:T(1,128)S(1)}) custom-call(bf16[64,128]{1,0:T(8,128)(2,1)} %img_in.1, bf16[4,2048]{1,0:T(4,128)(2,1)} %ref_in.1, bf16[1,4]{1,0:T(2,128)(2,1)} %bitcast.5, f32[1,32]{1,0:T(1,128)} %bitcast.6, s32[1,64]{1,0:T(1,128)} %bitcast.7), custom_call_target="tpu_custom_call" | custom-call | tf_op jit(solution)/shard_map/em/pallas_call | solution.py:470
  55.1 0.6 %copy.8 = f32[4,128]{1,0:T(4,128)} copy(f32[4,128]{1,0:T(4,128)S(1)} %get-tuple-element.6) | data formatting | bytes 4096
  55.7 0.5 slice_bitcast_fusion

commit v6 on v5

--- a/solution.py
+++ b/solution.py
@@ -281,13 +281,6 @@
 
         imgs[j] = img_ref[...]
 
-        @pl.when(owner)
-        def _():
-            ref_arrives(behind)
-            passed(0, 8, lambda copy: copy.start())
-            ref_arrives(ahead)
-            passed(8, 14, lambda copy: copy.start())
-
     last = ((z >= 7) & (z <= 11)).astype(jnp.int32)
 
     @functools.partial(loop, 0, 2)
@@ -299,6 +292,13 @@
         @pl.when(turn == 0)
         def _():
             send_out()
+
+    @pl.when(owner)
+    def _():
+        ref_arrives(behind)
+        passed(0, 8, lambda copy: copy.start())
+        ref_arrives(ahead)
+        passed(8, 14, lambda copy: copy.start())
 
     loop(1, PTCL, lambda d: image_copy(d, lax.rem(j + PTCL - d, PTCL)).wait_recv())
 

time: 56.4 us -> 52.4 us (0.929)
  Pallas kernels: 54.5 us -> 50.5 us
    pallas_call x1, Pallas kernels: 54.5 us -> 50.5 us  [on_device(): pl.pallas_call(em_kernel, out_shape=(VMEM((4, 128), F32), VMEM((1, 128),...]
where the time goes in v6:
time: 52.4 us; the launch traced here: 52.2 us
  Pallas kernels  50.5 us (96%)
  local copies, waits for them, and re-layouts  1.09 us (2%)
  between operations  0.64 us (1%)
    pallas_call x1, Pallas kernels, on_device(): pl.pallas_call(em_kernel, out_shape=(VMEM((4, 128), F32), VMEM((1, 128),...  50.5 us

profile of v6, /device:TPU:1, one launch (start us, length us, event | category | flops | bytes accessed | tf_op | source)
XLA Modules:
  0.0 52.2 jit_solution(15799937603381744540)
XLA Ops:
  0.6 50.5 %em.1 = (f32[4,128]{1,0:T(4,128)S(1)}, f32[1,128]{1,0:T(1,128)S(1)}) custom-call(bf16[64,128]{1,0:T(8,128)(2,1)} %img_in.1, bf16[4,2048]{1,0:T(4,128)(2,1)} %ref_in.1, bf16[1,4]{1,0:T(2,128)(2,1)} %bitcast.5, f32[1,32]{1,0:T(1,128)} %bitcast.6, s32[1,64]{1,0:T(1,128)} %bitcast.7), custom_call_target="tpu_custom_call" | custom-call | tf_op jit(solution)/shard_map/em/pallas_call | solution.py:470
  51.1 0.6 %copy.8 = f32[4,128]{1,0:T(4,128)} copy(f32[4,128]{1,0:T(4,128)S(1)} %get-tuple-element.6) | data formatting | bytes 4096
  51.7 0.5 slice_bitcast_fusion

commit v7 on v4

--- a/solution.py
+++ b/solution.py
@@ -81,9 +81,8 @@
 
 
 def join_matrix():
-    source, place = iota((256, 256), 0), iota((256, 256), 1)
-    inner = place % 128
-    return jnp.where(source == 128 * (inner % 2) + 64 * (place // 128) + inner // 2, 1.0, 0.0).astype(BF16)
+    source, place = iota((128, 128), 0), iota((128, 128), 1)
+    return jnp.where(source == 64 * (place % 2) + place // 2, 1.0, 0.0).astype(BF16)
 
 
 def pair_halves(first, second):
@@ -135,9 +134,9 @@
     img_in, ref_in, prior_in, focus_in, group_in,
     new_ref, share_ref,
     grid, tables, tables_t, picks, contrast, mrow, message, imgs, refs, flat, wide, refmat, turned, vals, square_lo,
-    stat, stats, spread, rows, parts, heap, outbox, inbox,
+    stat, stats, spread, rows, parts, heap,
     img_ref, ref_ref, prior_ref, focus_ref, group_ref, fetched,
-    img_send, img_recv, ref_send, ref_recv, stat_send, stat_recv, sum_send, sum_recv, out_send, out_recv,
+    img_send, img_recv, ref_send, ref_recv, stat_send, stat_recv, sum_send, sum_recv,
 ):
     c = lax.axis_index("cls")
     j = lax.axis_index("ptcl")
@@ -359,67 +358,68 @@
             points, tables_t[128 * STARTS[group] : 128 * STARTS[group + 1], :], preferred_element_type=F32
         )
         back = back[0:24] + back[24:48]
-        for part in range(3):
-            rows[pl.ds(8 * part + group, NK, stride=32), :] = back[NK * part : NK * (part + 1), :]
-    for i in range(24, 32):
-        rows[pl.ds(i, NK, stride=32), :] = jnp.broadcast_to(share, (NK, 128))
-    for k in range(NK):
-        parts[k] = rows[32 * k : 32 * (k + 1), :].astype(BF16)
-
-    def sum_copy(g):
-        return remote(parts.at[g], heap.at[c], sum_send.at[g], sum_recv.at[c], {"cls": 4 * g + home})
-
-    def out_copy(d):
-        target = lax.rem(j + d, PTCL)
-        return remote(outbox.at[target], inbox.at[lane], out_send.at[d], out_recv.at[lane], row_peer(d))
-
-    owners(lambda g: sum_copy(g).start())
+        real, imag, square = back[0:8], back[8:16], back[16:24]
+        low = iota((NK, 128), 1) < 64
+        rows[pl.ds(4 * group, NK, stride=32), :] = jnp.where(low, real, pltpu.roll(imag, 64, 1))
+        rows[pl.ds(4 * group + 1, NK, stride=32), :] = jnp.where(low, square, share)
+        rows[pl.ds(4 * group + 2, NK, stride=32), :] = jnp.where(low, pltpu.roll(real, 64, 1), imag)
+        rows[pl.ds(4 * group + 3, NK, stride=32), :] = jnp.where(low, pltpu.roll(square, 64, 1), share)
+    for i in range(NK * PTCL):
+        parts[i] = rows[2 * i : 2 * i + 2, :].astype(BF16)
+
+    def blocks(body):
+        @functools.partial(loop, 0, NK * PTCL)
+        def _(i):
+            step, b = i // PTCL, lax.rem(i, PTCL)
+            g = lax.rem(mine + NK // 2 + ((step + 1) // 2) * (2 * (step % 2) - 1) + NK, NK)
+
+            @pl.when((4 * g + home != c) | (b != j))
+            def _():
+                body(remote(
+                    parts.at[PTCL * g + b], heap.at[c, lane], sum_send.at[PTCL * g + b], sum_recv.at[c, lane],
+                    {"cls": 4 * g + home, "ptcl": b},
+                ))
+
+    blocks(lambda copy: copy.start())
 
     @pl.when(owner)
     def _():
-        heap[c] = parts[mine]
-
-        def arrive(d):
-            source = lax.rem(c + d, CLS)
-            remote(parts.at[0], heap.at[source], sum_send.at[0], sum_recv.at[source], {"cls": source}).wait_recv()
-
-        loop(1, CLS, arrive)
-        sums = lax.fori_loop(1, CLS, lambda i, t: t + heap[i].astype(F32), heap[0].astype(F32))
-        below = sums[16:24] + 1.0
-        planes = jnp.concatenate([sums[0:8] / below, sums[8:16] / below], axis=1)
-        high = planes.astype(BF16).astype(F32)
-        both = jnp.concatenate([high, planes - high], axis=0).astype(BF16)
-        joined = jnp.dot(both, join_matrix(), preferred_element_type=F32)
-        joined = joined[0:8] + joined[8:16]
-        for b in range(PTCL):
-            u, h = b // 2, b % 2
-            outbox[b] = jnp.where(
-                iota((8, 128), 0) == 0, joined[u : u + 1, 128 * h : 128 * (h + 1)], sums[24:25, :]
-            )
-        farthest(PTCL, lambda d: out_copy(d).start())
-        inbox[lane] = outbox[j]
-
-    @functools.partial(loop, 0, 4)
-    def _(i):
-        @pl.when(first + i != j)
-        def _():
-            remote(outbox.at[0], inbox.at[i], out_send.at[0], out_recv.at[i], row_peer(1)).wait_recv()
-
-    new_ref[...] = jnp.concatenate([inbox[i, 0:1, :] for i in range(4)], axis=0)
-    share_row = inbox[0, 1:2, :]
-    for i in range(1, 4):
-        share_row = jnp.where(iota((1, 128), 1) == i, inbox[i, 1:2, :], share_row)
-    share_ref[...] = share_row * (128.0 / 2048.0)
+        heap[c, lane] = parts[PTCL * mine + j]
 
     loop(1, PTCL, lambda d: image_copy(d, j).wait_send())
     loop(1, PTCL, lambda d: stat_copy(d, j).wait_send())
-    owners(lambda g: sum_copy(g).wait_send())
 
     @pl.when(owner)
     def _():
         loop(0, NEAR, lambda i: ref_copy(i).wait_send())
         loop(0, 14, lambda i: pass_on(i).wait_send())
-        loop(1, PTCL, lambda d: out_copy(d).wait_send())
+
+    blocks(lambda copy: copy.wait_send())
+
+    def arrive(i, total):
+        source = lax.rem(c + CLS + ((i + 1) // 2) * (1 - 2 * lax.rem(i, 2)), CLS)
+
+        @functools.partial(loop, 0, 4)
+        def _(t):
+            @pl.when((source != c) | (first + t != j))
+            def _():
+                remote(
+                    parts.at[0], heap.at[source, t], sum_send.at[0], sum_recv.at[source, t], row_peer(1)
+                ).wait_recv()
+
+        return total + heap[source].astype(F32)
+
+    sums = lax.fori_loop(0, CLS, arrive, jnp.zeros((4, 2, 128), F32))
+    top = jnp.concatenate([sums[i, 0:1, :] for i in range(4)], axis=0)
+    bottom = jnp.concatenate([sums[i, 1:2, :] for i in range(4)], axis=0)
+    turned_bottom = pltpu.roll(bottom, 64, 1)
+    value = top / (jnp.where(iota((4, 128), 1) < 64, bottom, turned_bottom) + 1.0)
+    high = value.astype(BF16).astype(F32)
+    both = jnp.concatenate([high, value - high], axis=0).astype(BF16)
+    joined = jnp.dot(both, join_matrix(), preferred_element_type=F32)
+    new_ref[...] = joined[0:4] + joined[4:8]
+    diagonal = iota((4, 128), 0) == iota((4, 128), 1)
+    share_ref[...] = jnp.sum(jnp.where(diagonal, turned_bottom, 0.0), axis=0, keepdims=True) * (128.0 / 2048.0)
 
 
 def on_device(images, references, log_prior, defocus, groups):
@@ -450,10 +450,8 @@
             VMEM((PTCL, 8, 128), F32),
             VMEM((3, ROWS, LANES), F32),
             VMEM((NK * 32, 128), F32),
-            VMEM((NK, 32, 128), BF16),
-            VMEM((CLS, 32, 128), BF16),
-            VMEM((PTCL, 8, 128), F32),
-            VMEM((4, 8, 128), F32),
+            VMEM((NK * PTCL, 2, 128), BF16),
+            VMEM((CLS, 4, 2, 128), BF16),
             VMEM((NB, 128), BF16),
             VMEM((4, 2 * PIX), BF16),
             VMEM((1, 4), BF16),
@@ -466,10 +464,8 @@
             dma((NK,)),
             dma((PTCL,)),
             dma((PTCL,)),
-            dma((NK,)),
-            dma((CLS,)),
-            dma((PTCL,)),
-            dma((4,)),
+            dma((NK * PTCL,)),
+            dma((CLS, 4)),
         ],
         compiler_params=pltpu.CompilerParams(
             collective_id=0, has_side_effects=True, vmem_limit_bytes=60 << 20

time: 52.1 us -> 52.5 us (level)
  no operation moved by 1% of the time
where the time goes in v7:
time: 52.5 us; the launch traced here: 52.3 us
  Pallas kernels  50.6 us (96%)
  local copies, waits for them, and re-layouts  1.09 us (2%)
  between operations  0.64 us (1%)
    pallas_call x1, Pallas kernels, on_device(): pl.pallas_call(em_kernel, out_shape=(VMEM((4, 128), F32), VMEM((1, 128),...  50.6 us

profile of v7, /device:TPU:1, one launch (start us, length us, event | category | flops | bytes accessed | tf_op | source)
XLA Modules:
  0.0 52.3 jit_solution(16528075336765867468)
XLA Ops:
  0.6 50.6 %em.1 = (f32[4,128]{1,0:T(4,128)S(1)}, f32[1,128]{1,0:T(1,128)S(1)}) custom-call(bf16[64,128]{1,0:T(8,128)(2,1)} %img_in.1, bf16[4,2048]{1,0:T(4,128)(2,1)} %ref_in.1, bf16[1,4]{1,0:T(2,128)(2,1)} %bitcast.5, f32[1,32]{1,0:T(1,128)} %bitcast.6, s32[1,64]{1,0:T(1,128)} %bitcast.7), custom_call_target="tpu_custom_call" | custom-call | tf_op jit(solution)/shard_map/em/pallas_call | solution.py:428
  51.2 0.6 %copy.8 = f32[4,128]{1,0:T(4,128)} copy(f32[4,128]{1,0:T(4,128)S(1)} %get-tuple-element.6) | data formatting | bytes 4096
  51.8 0.5 slice_bitcast_fusion

commit v8 on v4

--- a/solution.py
+++ b/solution.py
@@ -97,10 +97,6 @@
     return jnp.sum(jnp.where(iota((size, size), 0) == iota((size, size), 1), row, 0.0), axis=1, keepdims=True)
 
 
-def over_lanes(a, b):
-    return lax.dot_general(a, b, (((1,), (1,)), ((), ())), preferred_element_type=F32)
-
-
 def make_tables(grid, tables):
     place = iota((SIDE, 128), 0).astype(F32) - float(SIDE // 2)
     for r, patch, group, count, offset in BANDS:
@@ -134,7 +130,7 @@
 def em_kernel(
     img_in, ref_in, prior_in, focus_in, group_in,
     new_ref, share_ref,
-    grid, tables, tables_t, picks, contrast, mrow, message, imgs, refs, flat, wide, refmat, turned, vals, square_lo,
+    grid, tables, tables_t, picks, contrast, mrow, message, imgs, refs, flat, wide, refmat, turned, vals, square_lo, stack,
     stat, stats, spread, rows, parts, heap, outbox, inbox,
     img_ref, ref_ref, prior_ref, focus_ref, group_ref, fetched,
     img_send, img_recv, ref_send, ref_recv, stat_send, stat_recv, sum_send, sum_recv, out_send, out_recv,
@@ -283,6 +279,9 @@
         vals[2, pl.ds(row, NB), :] = high
         square_lo[pl.ds(row, NB), :] = (square - high.astype(F32)).astype(BF16)
 
+    for i, block in enumerate([vals[0], vals[1], vals[2], square_lo[...], vals[2]]):
+        stack[LANES * i : LANES * (i + 1), :] = block.T
+
     @functools.partial(owners)
     def _(g):
         @pl.when(jnp.logical_not(owner) | ((g != behind) & (g != ahead)))
@@ -309,22 +308,20 @@
         turned[1, NK * r : NK * (r + 1), 128 * patch : 128 * (patch + 1)] = both[NK:]
 
     real, imag = turned[0], turned[1]
-    match = over_lanes(real.astype(BF16), vals[0]) + over_lanes(imag.astype(BF16), vals[1])
-    power = real * real + imag * imag
+    power = -0.5 * (real * real + imag * imag)
     power_hi = power.astype(BF16)
     power_lo = (power - power_hi.astype(F32)).astype(BF16)
-    penalty = (
-        over_lanes(power_hi, vals[2]) + over_lanes(power_lo, vals[2]) + over_lanes(power_hi, square_lo[...])
-    )
+    left = jnp.concatenate([real.astype(BF16), imag.astype(BF16), power_hi, power_hi, power_lo], axis=1)
+    scores = jnp.dot(left, stack[...], preferred_element_type=F32)
     prior = jnp.concatenate([prior, prior], axis=1)
-    logits = match - 0.5 * penalty + jnp.concatenate([prior] * BASE, axis=0)
+    logits = scores + jnp.concatenate([prior] * BASE, axis=0)
     peak = jnp.max(logits, axis=0, keepdims=True)
     peak = jnp.maximum(peak[:, :128], peak[:, 128:])
     peak = jnp.maximum(peak, pltpu.roll(peak, 64, 1))
     total = jnp.sum(jnp.exp(logits - jnp.concatenate([peak, peak], axis=1)), axis=0, keepdims=True)
     total = total[:, :128] + total[:, 128:]
     total = total + pltpu.roll(total, 64, 1)
-    stat[...] = jnp.where(iota((8, 128), 0) == 0, peak, total)
+    stat[...] = jnp.where(iota((2, 128), 0) == 0, peak, total)
 
     def stat_copy(d, slot):
         return remote(stat, stats.at[slot], stat_send.at[d], stat_recv.at[d], row_peer(d))
@@ -332,6 +329,13 @@
     farthest(PTCL, lambda d: stat_copy(d, j).start())
     stats[j] = stat[...]
     turn_tables(tables, tables_t)
+    loop(1, PTCL, lambda d: image_copy(d, j).wait_send())
+
+    @pl.when(owner)
+    def _():
+        loop(0, NEAR, lambda i: ref_copy(i).wait_send())
+        loop(0, 14, lambda i: pass_on(i).wait_send())
+
     loop(1, PTCL, lambda d: stat_copy(d, lax.rem(j + PTCL - d, PTCL)).wait_recv())
     peaks = stats[:, 0:1, :]
     peak = jnp.max(peaks, axis=0)
@@ -374,17 +378,16 @@
         return remote(outbox.at[target], inbox.at[lane], out_send.at[d], out_recv.at[lane], row_peer(d))
 
     owners(lambda g: sum_copy(g).start())
-
-    @pl.when(owner)
-    def _():
-        heap[c] = parts[mine]
-
-        def arrive(d):
-            source = lax.rem(c + d, CLS)
+    loop(1, PTCL, lambda d: stat_copy(d, j).wait_send())
+
+    @pl.when(owner)
+    def _():
+        def arrive(i, total):
+            source = lax.rem(c + CLS + ((i + 2) // 2) * (1 - 2 * lax.rem(i, 2)), CLS)
             remote(parts.at[0], heap.at[source], sum_send.at[0], sum_recv.at[source], {"cls": source}).wait_recv()
-
-        loop(1, CLS, arrive)
-        sums = lax.fori_loop(1, CLS, lambda i, t: t + heap[i].astype(F32), heap[0].astype(F32))
+            return total + heap[source].astype(F32)
+
+        sums = lax.fori_loop(0, CLS - 1, arrive, parts[mine].astype(F32))
         below = sums[16:24] + 1.0
         planes = jnp.concatenate([sums[0:8] / below, sums[8:16] / below], axis=1)
         high = planes.astype(BF16).astype(F32)
@@ -394,10 +397,12 @@
         for b in range(PTCL):
             u, h = b // 2, b % 2
             outbox[b] = jnp.where(
-                iota((8, 128), 0) == 0, joined[u : u + 1, 128 * h : 128 * (h + 1)], sums[24:25, :]
+                iota((2, 128), 0) == 0, joined[u : u + 1, 128 * h : 128 * (h + 1)], sums[24:25, :]
             )
         farthest(PTCL, lambda d: out_copy(d).start())
         inbox[lane] = outbox[j]
+
+    owners(lambda g: sum_copy(g).wait_send())
 
     @functools.partial(loop, 0, 4)
     def _(i):
@@ -411,14 +416,9 @@
         share_row = jnp.where(iota((1, 128), 1) == i, inbox[i, 1:2, :], share_row)
     share_ref[...] = share_row * (128.0 / 2048.0)
 
-    loop(1, PTCL, lambda d: image_copy(d, j).wait_send())
-    loop(1, PTCL, lambda d: stat_copy(d, j).wait_send())
-    owners(lambda g: sum_copy(g).wait_send())
-
-    @pl.when(owner)
-    def _():
-        loop(0, NEAR, lambda i: ref_copy(i).wait_send())
-        loop(0, 14, lambda i: pass_on(i).wait_send())
+
+    @pl.when(owner)
+    def _():
         loop(1, PTCL, lambda d: out_copy(d).wait_send())
 
 
@@ -446,14 +446,15 @@
             VMEM((2, ROWS, LANES), F32),
             VMEM((3, 4 * NB, LANES), BF16),
             VMEM((4 * NB, LANES), BF16),
-            VMEM((8, 128), F32),
-            VMEM((PTCL, 8, 128), F32),
+            VMEM((5 * LANES, 4 * NB), BF16),
+            VMEM((2, 128), F32),
+            VMEM((PTCL, 2, 128), F32),
             VMEM((3, ROWS, LANES), F32),
             VMEM((NK * 32, 128), F32),
             VMEM((NK, 32, 128), BF16),
             VMEM((CLS, 32, 128), BF16),
-            VMEM((PTCL, 8, 128), F32),
-            VMEM((4, 8, 128), F32),
+            VMEM((PTCL, 2, 128), F32),
+            VMEM((4, 2, 128), F32),
             VMEM((NB, 128), BF16),
             VMEM((4, 2 * PIX), BF16),
             VMEM((1, 4), BF16),

time: 52.1 us -> 51.3 us (0.985)
  Pallas kernels: 50.1 us -> 49.4 us
    pallas_call x1, Pallas kernels: 50.1 us -> 49.4 us  [on_device(): pl.pallas_call(em_kernel, out_shape=(VMEM((4, 128), F32), VMEM((1, 128),...]
where the time goes in v8:
time: 51.3 us; the launch traced here: 51.1 us
  Pallas kernels  49.4 us (96%)
  local copies, waits for them, and re-layouts  1.09 us (2%)
  between operations  0.64 us (1%)
    pallas_call x1, Pallas kernels, on_device(): pl.pallas_call(em_kernel, out_shape=(VMEM((4, 128), F32), VMEM((1, 128),...  49.4 us

profile of v8, /device:TPU:1, one launch (start us, length us, event | category | flops | bytes accessed | tf_op | source)
XLA Modules:
  0.0 51.1 jit_solution(16586269379041617392)
XLA Ops:
  0.6 49.4 %em.1 = (f32[4,128]{1,0:T(4,128)S(1)}, f32[1,128]{1,0:T(1,128)S(1)}) custom-call(bf16[64,128]{1,0:T(8,128)(2,1)} %img_in.1, bf16[4,2048]{1,0:T(4,128)(2,1)} %ref_in.1, bf16[1,4]{1,0:T(2,128)(2,1)} %bitcast.5, f32[1,32]{1,0:T(1,128)} %bitcast.6, s32[1,64]{1,0:T(1,128)} %bitcast.7), custom_call_target="tpu_custom_call" | custom-call | tf_op jit(solution)/shard_map/em/pallas_call | solution.py:428
  50.0 0.6 %copy.8 = f32[4,128]{1,0:T(4,128)} copy(f32[4,128]{1,0:T(4,128)S(1)} %get-tuple-element.6) | data formatting | bytes 4096
  50.6 0.5 slice_bitcast_fusion

commit v9 on v8

--- a/solution.py
+++ b/solution.py
@@ -20,7 +20,6 @@
 CLS = 32
 PTCL = 16
 NK = 8
-NEAR = 17
 ROWS = BASE * NK
 NB = 64
 MESH = pl.DeviceIdType.MESH
@@ -183,14 +182,8 @@
         fetch.start()
 
     barrier = pltpu.get_barrier_semaphore()
-    z, x = c // 2, lax.rem(c, 2)
-
-    @functools.partial(owners)
-    def _(g):
-        @pl.when(lax.rem(2 * g + home // 2 - z + 20, 16) <= 8)
-        def _():
-            pl.semaphore_signal(barrier, inc=1, device_id={"cls": 4 * g + home}, device_id_type=MESH)
-
+    owners(lambda g: pl.semaphore_signal(
+        barrier, inc=1, device_id={"cls": 4 * g + home}, device_id_type=MESH))
     farthest(PTCL, lambda d: pl.semaphore_signal(barrier, inc=1, device_id=row_peer(d), device_id_type=MESH))
     for fetch in fetches:
         fetch.wait()
@@ -207,25 +200,14 @@
     grid_rows(grid)
     @pl.when(owner)
     def _():
-        pl.semaphore_wait(barrier, PTCL - 1 + NEAR)
+        pl.semaphore_wait(barrier, PTCL - 1 + CLS - 1)
 
     @pl.when(jnp.logical_not(owner))
     def _():
         pl.semaphore_wait(barrier, PTCL - 1)
 
-    def near(dz, flip):
-        return {"cls": 2 * lax.rem(z + dz + 16, 16) + lax.rem(x + flip, 2)}
-
-    def ref_copy(i):
-        target = near((4 - i // 4) * (1 - 2 * ((i // 2) % 2)), lax.rem(i + 1, 2))
-        return remote(message, refs.at[mine], ref_send.at[i], ref_recv.at[mine], target)
-
-    behind, ahead = lax.rem(mine + NK - 2, NK), lax.rem(mine + 2, NK)
-
-    def pass_on(i):
-        source = jnp.where(i < 8, behind, ahead)
-        target = near(jnp.where(i < 8, 4 - i // 2, i // 2 - 7), lax.rem(i, 2))
-        return remote(refs.at[source], refs.at[source], ref_send.at[NEAR + i], ref_recv.at[source], target)
+    def ref_copy(d):
+        return remote(message, refs.at[mine], ref_send.at[d], ref_recv.at[mine], column_peer(d))
 
     def ref_arrives(g):
         remote(message, refs.at[g], ref_send.at[0], ref_recv.at[g], column_peer(1)).wait_recv()
@@ -235,7 +217,7 @@
 
     @pl.when(owner)
     def _():
-        loop(0, NEAR, lambda i: ref_copy(i).start())
+        farthest(CLS, lambda d: ref_copy(d).start())
         refs[mine] = message[...]
 
     farthest(PTCL, lambda d: image_copy(d, j).start())
@@ -251,13 +233,6 @@
     contrast[...] = -(0.99499 * jnp.sin(phase) + 0.1 * jnp.cos(phase))
     make_picks(grid, picks)
 
-    @pl.when(owner)
-    def _():
-        ref_arrives(behind)
-        loop(0, 8, lambda i: pass_on(i).start())
-        ref_arrives(ahead)
-        loop(8, 14, lambda i: pass_on(i).start())
-
     loop(1, PTCL, lambda d: image_copy(d, lax.rem(j + PTCL - d, PTCL)).wait_recv())
 
     for u in range(8):
@@ -282,12 +257,7 @@
     for i, block in enumerate([vals[0], vals[1], vals[2], square_lo[...], vals[2]]):
         stack[LANES * i : LANES * (i + 1), :] = block.T
 
-    @functools.partial(owners)
-    def _(g):
-        @pl.when(jnp.logical_not(owner) | ((g != behind) & (g != ahead)))
-        def _():
-            ref_arrives(g)
-
+    owners(ref_arrives)
 
     flat[...] = jnp.dot(refs[...].reshape(NK * 32, 128), split, preferred_element_type=F32)
     for u in range(8):
@@ -333,8 +303,7 @@
 
     @pl.when(owner)
     def _():
-        loop(0, NEAR, lambda i: ref_copy(i).wait_send())
-        loop(0, 14, lambda i: pass_on(i).wait_send())
+        loop(1, CLS, lambda d: ref_copy(d).wait_send())
 
     loop(1, PTCL, lambda d: stat_copy(d, lax.rem(j + PTCL - d, PTCL)).wait_recv())
     peaks = stats[:, 0:1, :]

time: 51.3 us -> 54.3 us (1.058)
  Pallas kernels: 49.4 us -> 52.4 us
    pallas_call x1, Pallas kernels: 49.4 us -> 52.4 us  [on_device(): pl.pallas_call(em_kernel, out_shape=(VMEM((4, 128), F32), VMEM((1, 128),...]
where the time goes in v9:
time: 54.3 us; the launch traced here: 54.1 us
  Pallas kernels  52.4 us (97%)
  local copies, waits for them, and re-layouts  1.09 us (2%)
  between operations  0.64 us (1%)
    pallas_call x1, Pallas kernels, on_device(): pl.pallas_call(em_kernel, out_shape=(VMEM((4, 128), F32), VMEM((1, 128),...  52.4 us

profile of v9, /device:TPU:1, one launch (start us, length us, event | category | flops | bytes accessed | tf_op | source)
XLA Modules:
  0.0 54.1 jit_solution(966533610131019901)
XLA Ops:
  0.6 52.4 %em.1 = (f32[4,128]{1,0:T(4,128)S(1)}, f32[1,128]{1,0:T(1,128)S(1)}) custom-call(bf16[64,128]{1,0:T(8,128)(2,1)} %img_in.1, bf16[4,2048]{1,0:T(4,128)(2,1)} %ref_in.1, bf16[1,4]{1,0:T(2,128)(2,1)} %bitcast.5, f32[1,32]{1,0:T(1,128)} %bitcast.6, s32[1,64]{1,0:T(1,128)} %bitcast.7), custom_call_target="tpu_custom_call" | custom-call | tf_op jit(solution)/shard_map/em/pallas_call | solution.py:397
  53.1 0.6 %copy.8 = f32[4,128]{1,0:T(4,128)} copy(f32[4,128]{1,0:T(4,128)S(1)} %get-tuple-element.6) | data formatting | bytes 4096
  53.6 0.5 slice_bitcast_fusion

commit v10 on v8

--- a/solution.py
+++ b/solution.py
@@ -203,7 +203,9 @@
         mrow[m : m + 1, :] = chosen[:, 128 * m : 128 * (m + 1)]
     own_prior = jnp.sum(jnp.where(iota((1, 4), 1) == lane, prior_ref[...].astype(F32), 0.0), axis=1, keepdims=True)
     mrow[16:32, :] = jnp.broadcast_to(own_prior, (16, 128))
-    message[...] = mrow[...].astype(BF16)
+    for m in range(9):
+        message[m] = mrow[2 * m : 2 * m + 2, :].astype(BF16)
+    flat[...] = jnp.zeros_like(flat)
     grid_rows(grid)
     @pl.when(owner)
     def _():
@@ -289,7 +291,10 @@
             ref_arrives(g)
 
 
-    flat[...] = jnp.dot(refs[...].reshape(NK * 32, 128), split, preferred_element_type=F32)
+    for k in range(NK):
+        for m in range(9):
+            flat[32 * k + 2 * m : 32 * k + 2 * m + 2, :] = refs[k, m].astype(F32)
+    flat[...] = jnp.dot(flat[...].astype(BF16), split, preferred_element_type=F32)
     for u in range(8):
         real, imag = pair_halves(
             flat[pl.ds(2 * u, NK, stride=32), :], flat[pl.ds(2 * u + 1, NK, stride=32), :]
@@ -437,9 +442,9 @@
             VMEM((4 * PIX, LANES), BF16),
             VMEM((NB, LANES), F32),
             VMEM((32, 128), F32),
-            VMEM((32, 128), BF16),
+            VMEM((9, 2, 128), BF16),
             VMEM((PTCL, NB, 128), BF16),
-            VMEM((NK, 32, 128), BF16),
+            VMEM((NK, 9, 2, 128), BF16),
             VMEM((NK * 32, 128), F32),
             VMEM((2 * NB, PIX), BF16),
             VMEM((2 * NK, PIX), BF16),

time: 51.3 us -> 51.5 us (level)
  no operation moved by 1% of the time
where the time goes in v10:
time: 51.5 us; the launch traced here: 51.3 us
  Pallas kernels  49.6 us (96%)
  local copies, waits for them, and re-layouts  1.09 us (2%)
  between operations  0.64 us (1%)
    pallas_call x1, Pallas kernels, on_device(): pl.pallas_call(em_kernel, out_shape=(VMEM((4, 128), F32), VMEM((1, 128),...  49.6 us

profile of v10, /device:TPU:1, one launch (start us, length us, event | category | flops | bytes accessed | tf_op | source)
XLA Modules:
  0.0 51.3 jit_solution(17818486135170586997)
XLA Ops:
  0.6 49.6 %em.1 = (f32[4,128]{1,0:T(4,128)S(1)}, f32[1,128]{1,0:T(1,128)S(1)}) custom-call(bf16[64,128]{1,0:T(8,128)(2,1)} %img_in.1, bf16[4,2048]{1,0:T(4,128)(2,1)} %ref_in.1, bf16[1,4]{1,0:T(2,128)(2,1)} %bitcast.5, f32[1,32]{1,0:T(1,128)} %bitcast.6, s32[1,64]{1,0:T(1,128)} %bitcast.7), custom_call_target="tpu_custom_call" | custom-call | tf_op jit(solution)/shard_map/em/pallas_call | solution.py:433
  50.3 0.6 %copy.8 = f32[4,128]{1,0:T(4,128)} copy(f32[4,128]{1,0:T(4,128)S(1)} %get-tuple-element.6) | data formatting | bytes 4096
  50.8 0.5 slice_bitcast_fusion

commit v11 on v8

--- a/solution.py
+++ b/solution.py
@@ -253,10 +253,25 @@
 
     @pl.when(owner)
     def _():
-        ref_arrives(behind)
-        loop(0, 8, lambda i: pass_on(i).start())
-        ref_arrives(ahead)
-        loop(8, 14, lambda i: pass_on(i).start())
+        def pass_behind():
+            ref_arrives(behind)
+            loop(0, 8, lambda i: pass_on(i).start())
+
+        def pass_ahead():
+            ref_arrives(ahead)
+            loop(8, 14, lambda i: pass_on(i).start())
+
+        other_first = lax.rem(z + 4, 16) < 8
+
+        @pl.when(other_first)
+        def _():
+            pass_ahead()
+
+        pass_behind()
+
+        @pl.when(jnp.logical_not(other_first))
+        def _():
+            pass_ahead()
 
     loop(1, PTCL, lambda d: image_copy(d, lax.rem(j + PTCL - d, PTCL)).wait_recv())
 

time: 51.3 us -> 51.8 us (level)
    pallas_call x1, Pallas kernels: 49.4 us -> 49.9 us  [on_device(): pl.pallas_call(em_kernel, out_shape=(VMEM((4, 128), F32), VMEM((1, 128),...]
where the time goes in v11:
time: 51.8 us; the launch traced here: 51.7 us
  Pallas kernels  49.9 us (96%)
  local copies, waits for them, and re-layouts  1.09 us (2%)
  between operations  0.64 us (1%)
    pallas_call x1, Pallas kernels, on_device(): pl.pallas_call(em_kernel, out_shape=(VMEM((4, 128), F32), VMEM((1, 128),...  49.9 us

profile of v11, /device:TPU:1, one launch (start us, length us, event | category | flops | bytes accessed | tf_op | source)
XLA Modules:
  0.0 51.7 jit_solution(9992803623157882100)
XLA Ops:
  0.6 49.9 %em.1 = (f32[4,128]{1,0:T(4,128)S(1)}, f32[1,128]{1,0:T(1,128)S(1)}) custom-call(bf16[64,128]{1,0:T(8,128)(2,1)} %img_in.1, bf16[4,2048]{1,0:T(4,128)(2,1)} %ref_in.1, bf16[1,4]{1,0:T(2,128)(2,1)} %bitcast.5, f32[1,32]{1,0:T(1,128)} %bitcast.6, s32[1,64]{1,0:T(1,128)} %bitcast.7), custom_call_target="tpu_custom_call" | custom-call | tf_op jit(solution)/shard_map/em/pallas_call | solution.py:443
  50.6 0.6 %copy.8 = f32[4,128]{1,0:T(4,128)} copy(f32[4,128]{1,0:T(4,128)S(1)} %get-tuple-element.6) | data formatting | bytes 4096
  51.1 0.5 slice_bitcast_fusion
